TPU v7x, 32 devices: a whole 2x2x4 slice. The times are simulated.
32 devices in a mesh: crop: 1, res: 32 (over z, y, x, core).
Axes of the slice: x: 2, y: 2, z: 4, core: 2. Of those that a mesh axis runs over, the one named last changes fastest.
Arguments:
- homolog_symbol_ids: int32 [64, 128], P(('crop', 'res')), may hold values from 0 to 22
- residue_attend_mask: int32 [128], P('crop'), may hold values 0 or 1
- alignment_state: bfloat16 [64, 128, 256], P(('crop', 'res')), may hold values from -6 to 6
- pair: bfloat16 [128, 128, 128], P(('crop', 'res')), may hold values from -6 to 6
- symbol_lookup_matrix: bfloat16 [23, 256], replicated, may hold values from -3 to 3
- pair_bias_weight: bfloat16 [128, 8], replicated, may hold values from -0.5 to 0.5
- row_projection_weight: bfloat16 [256, 1024], replicated, may hold values from -8 to 8
- horizontal_readout_matrix: bfloat16 [256, 256], replicated, may hold values from -0.375 to 0.375
- column_projection_weight: bfloat16 [256, 1024], replicated, may hold values from -8 to 8
- vertical_readout_matrix: bfloat16 [256, 256], replicated, may hold values from -0.375 to 0.375
- product_factor_matrices: bfloat16 [256, 64], replicated, may hold values from -0.375 to 0.375
- outer_output_weight: bfloat16 [1024, 128], replicated, may hold values from -1.5 to 1.5
- triangle_input_weight: bfloat16 [128, 640], replicated, may hold values from -0.5 to 0.5
- triangle_output_weight: bfloat16 [128, 128], replicated, may hold values from -0.5 to 0.5
Outputs:
- alignment_output: bfloat16 [64, 128, 256], P('crop', 'res')
- pair_output: bfloat16 [128, 128, 128], P(('crop', 'res'))
All inputs are finite; a program needn't handle non-finite values.
Results may differ from a plain program's by a relative error of at most 0.013.
Values may be sent and summed in bfloat16 or wider, within the bound.
A program may use at most 64 MiB of HBM per device.

v0:
```python
import functools

import jax
import jax.numpy as jnp
from jax import lax
from jax.experimental import pallas as pl
from jax.experimental.pallas import tpu as pltpu
from jax.sharding import PartitionSpec as P

EPSILON = 1e-05
MESH = pl.DeviceIdType.MESH


def exchange_kernel(count, gather, source, landing, send_sem, recv_sem):
    me = lax.axis_index("res")
    barrier = pltpu.get_barrier_semaphore()

    @pl.loop(1, count)
    def _(step):
        pl.semaphore_signal(
            barrier,
            inc=1,
            device_id={"res": lax.rem(me + step, count)},
            device_id_type=MESH,
        )

    landing[me] = source[...] if gather else source[me]
    pl.semaphore_wait(barrier, count - 1)

    @pl.loop(1, count)
    def _(step):
        peer = lax.rem(me + step, count)
        pltpu.make_async_remote_copy(
            src_ref=source if gather else source.at[peer],
            dst_ref=landing.at[me],
            send_sem=send_sem,
            recv_sem=recv_sem,
            device_id={"res": peer},
            device_id_type=MESH,
        ).start()

    others = landing.at[pl.ds(0, count - 1)]
    pltpu.make_async_copy(others, others, recv_sem).wait()
    pltpu.make_async_copy(others, others, send_sem).wait()


def exchange(operand, gather, number):
    count = lax.axis_size("res")
    extent = operand.shape if gather else operand.shape[1:]
    return pl.pallas_call(
        functools.partial(exchange_kernel, count, gather),
        out_shape=jax.ShapeDtypeStruct((count,) + extent, operand.dtype),
        in_specs=[pl.BlockSpec(memory_space=pltpu.VMEM)],
        out_specs=pl.BlockSpec(memory_space=pltpu.VMEM),
        scratch_shapes=[pltpu.SemaphoreType.DMA, pltpu.SemaphoreType.DMA],
        compiler_params=pltpu.CompilerParams(
            collective_id=number, has_side_effects=True
        ),
    )(operand)


def layer_normalized(input_rows, axis):
    average = jnp.mean(input_rows, axis, keepdims=True)
    centred = input_rows - average
    spread = jnp.mean(centred * centred, axis, keepdims=True)
    return centred * lax.rsqrt(spread + EPSILON)


def split_proj(input_rows, weight, head_count):
    channels = weight.shape[0]
    head_size = channels // head_count
    projected = jnp.einsum("blc,ce->ble", input_rows, weight, preferred_element_type=jnp.float32)
    lead = projected.shape[:2]
    query_tensor = (
        (projected[..., :channels] * head_size ** (-0.5))
        .astype(jnp.bfloat16)
        .reshape(lead + (head_count, head_size))
    )
    key_tensor = (
        projected[..., channels : 2 * channels]
        .astype(jnp.bfloat16)
        .reshape(lead + (head_count, head_size))
    )
    value_tensor = (
        projected[..., 2 * channels : 3 * channels]
        .astype(jnp.bfloat16)
        .reshape(lead + (head_count, head_size))
    )
    gate_values = projected[..., 3 * channels :]
    return (query_tensor, key_tensor, value_tensor, gate_values)


def attention_block_fn(query_tensor, key_tensor, value_tensor, gate_values, extra_bias, out_weight):
    scores = (
        jnp.einsum("bqhd,bkhd->bhqk", query_tensor, key_tensor, preferred_element_type=jnp.float32)
        + extra_bias
    )
    row_top = jnp.max(scores, -1, keepdims=True)
    exp_scores = jnp.exp(scores - row_top)
    weights = (exp_scores / jnp.sum(exp_scores, -1, keepdims=True)).astype(jnp.bfloat16)
    mixed = jnp.einsum("bhqk,bkhd->bqhd", weights, value_tensor, preferred_element_type=jnp.float32)
    gated = (jax.nn.sigmoid(gate_values) * mixed.reshape(gate_values.shape)).astype(jnp.bfloat16)
    return jnp.einsum("bqc,ce->bqe", gated, out_weight, preferred_element_type=jnp.float32)


def shards(
    homolog_symbol_ids,
    residue_attend_mask,
    alignment_state,
    pair,
    symbol_lookup_matrix,
    pair_bias_weight,
    row_projection_weight,
    horizontal_readout_matrix,
    column_projection_weight,
    vertical_readout_matrix,
    product_factor_matrices,
    outer_output_weight,
    triangle_input_weight,
    triangle_output_weight,
):
    residue_count = lax.axis_size("res")
    sequence_total = alignment_state.shape[0] * residue_count
    res_local = pair.shape[0]
    chain_total = pair.shape[1]
    pair_chan = pair.shape[2]
    owner_chan = pair_chan // residue_count
    outer_chan = product_factor_matrices.shape[1] // 2
    head_count = pair_bias_weight.shape[1]
    token_class_count = symbol_lookup_matrix.shape[0]
    one_hot_tokens = (
        homolog_symbol_ids[:, :, None]
        == jnp.arange(token_class_count, dtype=jnp.int32)[None, None, :]
    ).astype(jnp.bfloat16)
    alignment_initial = alignment_state.astype(jnp.float32) + jnp.einsum(
        "kly,yb->klb", one_hot_tokens, symbol_lookup_matrix, preferred_element_type=jnp.float32
    )
    pair_normed = layer_normalized(pair.astype(jnp.float32), -1).astype(jnp.bfloat16)
    bias_local = jnp.einsum(
        "ijc,ch->hij", pair_normed, pair_bias_weight, preferred_element_type=jnp.float32
    ).astype(jnp.bfloat16)
    mask_bias = (residue_attend_mask.astype(jnp.float32) - 1.0) * 10000.0
    row_input = layer_normalized(alignment_initial, -1).astype(jnp.bfloat16)
    query_tensor, key_tensor, value_tensor, gate_values = split_proj(
        row_input, row_projection_weight, head_count
    )
    bias_all = exchange(bias_local.reshape(-1, chain_total), True, 0)
    bias_all = jnp.swapaxes(
        bias_all.reshape(residue_count, head_count, res_local, chain_total), 0, 1
    ).reshape(head_count, chain_total, chain_total)
    extra_bias = bias_all.astype(jnp.float32)[None] + mask_bias[None, None, None, :]
    row_attention_update = attention_block_fn(
        query_tensor, key_tensor, value_tensor, gate_values, extra_bias, horizontal_readout_matrix
    )
    alignment_after_rows = (alignment_initial + row_attention_update).astype(jnp.bfloat16)
    seqs_local, channels = alignment_state.shape[0], alignment_state.shape[2]
    outgoing = jnp.swapaxes(
        alignment_after_rows.reshape(seqs_local, residue_count, res_local, channels), 0, 1
    )
    alignment_columns = exchange(
        outgoing.reshape(residue_count, -1, 2 * channels), False, 1
    ).reshape(sequence_total, res_local, channels)
    column_start = jnp.swapaxes(alignment_columns, 0, 1).astype(jnp.float32)
    col_in = layer_normalized(column_start, -1).astype(jnp.bfloat16)
    col_queries, col_keys, col_values, col_gating = split_proj(
        col_in, column_projection_weight, head_count
    )
    alignment_after_columns = column_start + attention_block_fn(
        col_queries, col_keys, col_values, col_gating, jnp.float32(0.0), vertical_readout_matrix
    )
    alignment_output = jnp.swapaxes(alignment_after_columns, 0, 1).astype(jnp.bfloat16)
    outer_input = layer_normalized(alignment_after_columns, -1).astype(jnp.bfloat16)
    factor_ab = jnp.einsum(
        "rsc,ce->rse", outer_input, product_factor_matrices, preferred_element_type=jnp.float32
    )
    left = factor_ab[..., :outer_chan].astype(jnp.bfloat16)
    latter_factor = (
        factor_ab[..., outer_chan:]
        .astype(jnp.bfloat16)
        .reshape(res_local, sequence_total * outer_chan)
    )
    piece = exchange(latter_factor.reshape(-1, 128), True, 2)
    count = chain_total
    right_rows = piece.reshape(count, sequence_total, outer_chan)
    cross_product_result = (
        jnp.einsum("isc,jsd->ijcd", left, right_rows, preferred_element_type=jnp.float32)
        / sequence_total
    ).astype(jnp.bfloat16)
    update = jnp.einsum(
        "ije,ez->ijz",
        cross_product_result.reshape(res_local, count, outer_chan * outer_chan),
        outer_output_weight,
        preferred_element_type=jnp.float32,
    )
    pair_one = pair.astype(jnp.float32) + update
    tri_normed = layer_normalized(pair_one, -1).astype(jnp.bfloat16)
    factors = jnp.einsum(
        "ijc,ce->eij",
        tri_normed,
        triangle_input_weight[:, : 4 * pair_chan],
        preferred_element_type=jnp.float32,
    )
    gate_out = jnp.einsum(
        "ijc,ce->ije",
        tri_normed,
        triangle_input_weight[:, 4 * pair_chan :],
        preferred_element_type=jnp.float32,
    )
    left_f = (jax.nn.sigmoid(factors[pair_chan : 2 * pair_chan]) * factors[:pair_chan]).astype(
        jnp.bfloat16
    )
    right_f = (
        jax.nn.sigmoid(factors[3 * pair_chan :]) * factors[2 * pair_chan : 3 * pair_chan]
    ).astype(jnp.bfloat16)
    left_f = left_f.reshape(residue_count, owner_chan, res_local, chain_total)
    right_f = right_f.reshape(residue_count, owner_chan, res_local, chain_total)
    both = jnp.concatenate([left_f, right_f], axis=1)
    both = exchange(both.reshape(residue_count, -1, chain_total), False, 3)
    both = both.reshape(residue_count, 2, owner_chan, res_local, chain_total)
    both = jnp.transpose(both, (1, 2, 0, 3, 4)).reshape(
        2, owner_chan, chain_total, chain_total
    )
    combined = jnp.einsum(
        "cik,cjk->cij", both[0], both[1], preferred_element_type=jnp.float32
    ).astype(jnp.bfloat16)
    combined = jnp.swapaxes(
        combined.reshape(owner_chan, residue_count, res_local, chain_total), 0, 1
    )
    back_rows = exchange(combined.reshape(residue_count, -1, chain_total), False, 4)
    back_rows = back_rows.reshape(pair_chan, res_local, chain_total)
    comb_normed = layer_normalized(back_rows.astype(jnp.float32), 0).astype(jnp.bfloat16)
    tri_update = jnp.einsum(
        "cij,cz->ijz", comb_normed, triangle_output_weight, preferred_element_type=jnp.float32
    )
    pair_output = (pair_one + jax.nn.sigmoid(gate_out) * tri_update).astype(jnp.bfloat16)
    return (alignment_output, pair_output)


def solution(mesh):
    placed = (
        P(("crop", "res"), None),
        P("crop"),
        P(("crop", "res"), None, None),
        P(("crop", "res"), None, None),
        P(),
        P(),
        P(),
        P(),
        P(),
        P(),
        P(),
        P(),
        P(),
        P(),
    )
    return jax.shard_map(
        shards,
        mesh=mesh,
        in_specs=placed,
        out_specs=(P("crop", "res", None), P(("crop", "res"), None, None)),
        check_vma=False,
    )
```

profile of v0, /device:TPU:0, one launch (start us, length us, event | category | flops | bytes accessed | tf_op | source)
XLA Modules:
  0.0 102.5 jit_solution(10808646492546525615)
XLA Ops:
  0.7 0.7 add_multiply_fusion
  1.4 1.0 copy.50
  2.5 0.1 fusion.22
  2.5 0.8 fusion.13
  3.4 0.6 copy.52
  4.0 13.1 %shard_map.149 = bf16[32,32,128]{2,1,0:T(8,128)(2,1)} custom-call(bf16[32,128]{1,0:T(8,128)(2,1)} %bitcast.156), custom_call_target="tpu_custom_call" | custom-call | tf_op jit(solution)/shard_map/pallas_call | solution.py:50
  17.1 1.0 copy.53
  18.2 0.2 copy.54
  18.4 0.3 fusion.82
  18.8 0.2 multiply_reduce_fusion.4
  19.0 0.4 fusion.83
  19.4 0.1 copy.49
  19.5 0.8 copy.47
  20.3 0.1 copy.48
  20.4 0.6 copy-done.2
  21.1 0.5 fusion.84
  21.6 1.3 %convolution_add_fusion = f32[2,8,128,128]{2,3,1,0:T(8,128)S(1)} fusion(bf16[2,128,8,32]{1,3,2,0:T(8,128)(2,1)} %bitcast.144, bf16[2,128,8,32]{1,3,2,0:T(8,128)(2,1)} %bitcast.142, f32[8,128,128]{1,2,0:T(8,128)S(1)} %copy.54), kind=kOutput, calls=%fused_computation.9 | convolution fusion | flops 17039360 | bytes 1835008 | tf_op jit(solution)/shard_map/bqhd,bkhd->bhqk/dot_general | solution.py:95
  22.9 1.2 %fusion.19 = f32[2,8,32,128]{3,2,1,0:T(8,128)S(1)} fusion(bf16[2,128,8,32]{1,3,2,0:T(8,128)(2,1)} %bitcast.155, f32[2,8,128]{2,1,0:T(8,128)S(1)} %fusion.84, f32[2,8,128,128]{2,3,1,0:T(8,128)S(1)} %convolution_add_fusion), kind=kOutput, calls=%fused_computation.33 | convolution fusion | flops 17565824 | bytes 1449984 | tf_op jit(solution)/shard_map/bhqk,bkhd->bqhd/dot_general | solution.py:101
  24.1 0.1 copy.56
  24.3 1.1 %fusion.11 = bf16[2,128,256]{2,1,0:T(8,128)(2,1)S(1)} fusion(f32[2,128,256]{2,1,0:T(8,128)S(1)} %get-tuple-element.15, f32[2,128,256]{2,1,0:T(8,128)S(1)} %copy.56, f32[2,128,1024]{2,1,0:T(8,128)S(1)} %get-tuple-element.17, bf16[256,256]{1,0:T(8,128)(2,1)} %param.21), kind=kOutput, calls=%fused_computation.19 | convolution fusion | flops 34013184 | bytes 1048576 | tf_op jit(solution)/shard_map/bqc,ce->bqe/dot_general | solution.py:103
  25.5 0.7 reshape.173.source
  26.3 10.9 %shard_map.150 = bf16[32,4,512]{2,1,0:T(4,128)(2,1)} custom-call(bf16[32,4,512]{2,1,0:T(4,128)(2,1)} %reshape.173.source), custom_call_target="tpu_custom_call" | custom-call | tf_op jit(solution)/shard_map/pallas_call | solution.py:50
  37.2 1.0 reshape.188
  38.2 0.1 bitcast_reduce_fusion
  38.3 0.2 multiply_reduce_fusion.3
  38.5 0.3 fusion.85
  38.9 0.2 copy.61
  39.1 0.2 copy.60
  39.3 0.5 fusion.86
  39.8 0.8 copy.59
  40.6 0.3 fusion.88
  41.0 1.3 %fusion.18 = f32[4,8,32,64]{3,2,1,0:T(8,128)S(1)} fusion(bf16[4,64,8,32]{1,3,2,0:T(8,128)(2,1)} %bitcast.153, f32[4,8,64]{2,1,0:T(8,128)S(1)} %fusion.86, f32[4,8,64,64]{2,3,1,0:T(8,128)S(1)} %fusion.88), kind=kOutput, calls=%fused_computation.32 | convolution fusion | flops 8783935 | bytes 925696 | tf_op jit(solution)/shard_map/bhqk,bkhd->bqhd/dot_general | solution.py:101
  42.3 0.2 copy.63
  42.5 1.1 %fusion.43 = (bf16[64,4,256]{2,0,1:T(8,128)(2,1)S(1)}, f32[4,64,256]{2,1,0:T(8,128)S(1)}) fusion(f32[64,4,256]{2,1,0:T(4,128)S(1)} %reshape.188, bf16[256,256]{1,0:T(8,128)(2,1)} %param.23, f32[4,64,256]{2,1,0:T(8,128)S(1)} %copy.63, f32[4,64,1024]{2,1,0:T(8,128)S(1)} %get-tuple-element.19), kind=kOutput, calls=%fused_computation.69 | convolution fusion | flops 34013184 | bytes 1310720 | tf_op jit(solution)/shard_map/bqc,ce->bqe/dot_general | solution.py:103
  43.6 0.8 copy.81
  44.4 0.1 fusion.78
  44.5 0.2 multiply_reduce_fusion.2
  44.7 0.3 convolution_convert_fusion.1
  45.0 0.6 copy-done.4
  45.6 0.1 copy.65
  45.7 0.7 reshape_reshape.3.source
  46.4 16.3 %shard_map.151 = bf16[32,64,128]{2,1,0:T(8,128)(2,1)} custom-call(bf16[64,128]{1,0:T(8,128)(2,1)} %reshape_reshape.3.source), custom_call_target="tpu_custom_call" | custom-call | tf_op jit(solution)/shard_map/pallas_call | solution.py:50
  62.7 2.7 %reshape.178 = bf16[128,64,32]{2,1,0:T(8,128)(2,1)S(1)} reshape(bf16[32,64,128]{2,1,0:T(8,128)(2,1)} %shard_map.151) | data formatting | bytes 1048576 | tf_op jit(solution)/shard_map/reshape | solution.py:184
  65.4 2.6 %copy.86 = bf16[128,64,32,1]{0,1,3,2:T(8,128)(2,1)S(1)} copy(bf16[128,64,32,1]{2,1,0,3:T(8,128)(2,1)S(1)} %bitcast.130) | data formatting | bytes 1048576 | tf_op jit(solution)/shard_map/reshape | solution.py:184
  68.1 0.4 fusion.6
  68.5 0.7 copy.67
  69.2 0.4 fusion.87
  69.6 0.3 fusion.10
  69.9 0.3 convolution_bitcast_fusion
  70.2 0.1 fusion.28
  70.4 0.1 copy.73
  70.5 0.1 copy.74
  70.7 0.1 pad_maximum_fusion
  70.8 0.9 copy.75
  71.7 14.2 %shard_map.152 = bf16[32,32,128]{2,1,0:T(8,128)(2,1)} custom-call(bf16[32,32,128]{2,1,0:T(8,128)(2,1)} %bitcast.136), custom_call_target="tpu_custom_call" | custom-call | tf_op jit(solution)/shard_map/pallas_call | solution.py:50
  85.9 1.1 %fusion.81 = (bf16[1,4,32,4,128]{4,3,1,0,2:T(4,128)(2,1)S(1)}, bf16[1,4,32,4,128]{4,3,1,0,2:T(4,128)(2,1)S(1)}) fusion(bf16[2,4,32,4,128]{4,3,1,0,2:T(4,128)(2,1)} %bitcast.135), kind=kLoop, calls=%fused_computation.133 | loop fusion | bytes 524288 | tf_op jit(solution)/shard_map/slice | solution.py:224
  87.1 0.2 convolution_convert_fusion
  87.3 0.7 copy.78
  88.0 10.9 %shard_map.153 = bf16[32,16,128]{2,1,0:T(8,128)(2,1)} custom-call(bf16[32,16,128]{2,1,0:T(8,128)(2,1)} %bitcast.150), custom_call_target="tpu_custom_call" | custom-call | tf_op jit(solution)/shard_map/pallas_call | solution.py:50
  98.9 1.1 %convert_reduce_fusion.1 = f32[4,128]{1,0:T(4,128)S(1)} fusion(bf16[128,4,128]{2,1,0:T(4,128)(2,1)} %bitcast.132), kind=kLoop, calls=%fused_computation.103 | loop fusion | flops 130560 | bytes 133120 | tf_op jit(solution)/shard_map/reduce_sum | solution.py:63
  100.0 1.0 %copy.79 = f32[128,4,128]{0,2,1:T(8,128)S(1)} copy(bf16[128,4,128]{2,1,0:T(4,128)(2,1)} %bitcast.133) | data formatting | bytes 393216 | tf_op jit(solution)/shard_map/convert_element_type | solution.py:231
  101.0 0.2 multiply_reduce_fusion
  101.3 0.4 fusion.12
  101.7 0.8 copy.82
  (48 shorter events, 0.5 us)
Async XLA Ops:
  0.6 18.3 %copy-start = (bf16[256,1024]{1,0:T(8,128)(2,1)S(1)}, bf16[256,1024]{1,0:T(8,128)(2,1)}, u32[]{:S(2)}) copy-start(bf16[256,1024]{1,0:T(8,128)(2,1)} %param.20) | copy-start | bytes 1572868
  0.6 17.8 %copy-start.11 = (bf16[23,256]{1,0:T(8,128)(2,1)S(1)}, bf16[23,256]{1,0:T(8,128)(2,1)}, u32[]{:S(2)}) copy-start(bf16[23,256]{1,0:T(8,128)(2,1)} %param.18) | copy-start | bytes 35332
  0.7 17.8 %copy-start.7 = (bf16[2,128,256]{2,1,0:T(8,128)(2,1)S(1)}, bf16[2,128,256]{2,1,0:T(8,128)(2,1)}, u32[]{:S(2)}) copy-start(bf16[2,128,256]{2,1,0:T(8,128)(2,1)} %param.16) | copy-start | bytes 393220
  0.7 17.8 %copy-start.12 = (s32[2,128]{1,0:T(2,128)S(1)}, s32[2,128]{1,0:T(2,128)}, u32[]{:S(2)}) copy-start(s32[2,128]{1,0:T(2,128)} %param.14) | copy-start | bytes 3076
  19.5 0.9 copy-start.1
  20.4 0.7 copy-start.2
  24.1 14.4 %copy-start.3 = (bf16[256,1024]{1,0:T(8,128)(2,1)S(1)}, bf16[256,1024]{1,0:T(8,128)(2,1)}, u32[]{:S(2)}) copy-start(bf16[256,1024]{1,0:T(8,128)(2,1)} %param.22) | copy-start | bytes 1572868
  42.3 2.4 %copy-start.9 = (bf16[256,64]{0,1:T(8,128)(2,1)S(1)}, bf16[256,64]{0,1:T(8,128)(2,1)}, u32[]{:S(2)}) copy-start(bf16[256,64]{0,1:T(8,128)(2,1)} %param.24) | copy-start | bytes 98308
  45.0 0.6 copy-start.4
  62.7 5.3 %copy-start.5 = (bf16[4,64,64]{1,2,0:T(8,128)(2,1)S(1)}, bf16[4,64,64]{1,2,0:T(8,128)(2,1)}, u32[]{:S(2)}) copy-start(bf16[4,64,64]{1,2,0:T(8,128)(2,1)} %copy-done.4) | copy-start | bytes 98308
  68.0 1.1 %copy-start.6 = (bf16[1024,128]{1,0:T(8,128)(2,1)S(1)}, bf16[1024,128]{1,0:T(8,128)(2,1)}, u32[]{:S(2)}) copy-start(bf16[1024,128]{1,0:T(8,128)(2,1)} %param.25) | copy-start | bytes 786436
  68.5 1.2 %copy-start.8 = (bf16[128,640]{1,0:T(8,128)(2,1)S(1)}, bf16[128,640]{1,0:T(8,128)(2,1)}, u32[]{:S(2)}) copy-start(bf16[128,640]{1,0:T(8,128)(2,1)} %param.26) | copy-start | bytes 491524
  70.7 30.6 %copy-start.10 = (bf16[128,128]{1,0:T(8,128)(2,1)S(1)}, bf16[128,128]{1,0:T(8,128)(2,1)}, u32[]{:S(2)}) copy-start(bf16[128,128]{1,0:T(8,128)(2,1)} %param.27) | copy-start | bytes 98308
where the time goes:
time: 103 us; the launch traced here: 102 us
  Pallas kernels  65.4 us (63%)
  local copies, waits for them, and re-layouts  20.9 us (20%)
  matrix products  11.5 us (11%)
  other arithmetic  3.39 us (3%)
  between operations  1.21 us (1%)
    pallas_call x5, Pallas kernels, exchange(): pl.pallas_call(functools.partial(exchange_kernel, count, gather), out_sha...  65.4 us
    reshape x2, local copies, waits for them, and re-layouts, shards(): right_rows = piece.reshape(count, sequence_total, outer_chan)  5.29 us
    unnamed x29, local copies, waits for them, and re-layouts  3.88 us
    dot_general x2, matrix products, attention_block_fn(): jnp.einsum('bhqk,bkhd->bqhd', weights, value_tensor, preferred_element_ty...  2.55 us
    dot_general x2, matrix products, attention_block_fn(): jnp.einsum('bqc,ce->bqe', gated, out_weight, preferred_element_type=jnp.f...  2.27 us

commit v1 on v0

v1 whole, which is shorter than its diff:
```python
import functools

import jax
import jax.numpy as jnp
from jax import lax
from jax.experimental import pallas as pl
from jax.experimental.pallas import tpu as pltpu
from jax.sharding import PartitionSpec as P

EPSILON = 1e-05
MESH = pl.DeviceIdType.MESH
F32 = jnp.float32
BF16 = jnp.bfloat16

NN = (((1,), (0,)), ((), ()))
NT = (((1,), (1,)), ((), ()))
TN = (((0,), (0,)), ((), ()))


def dot(a, b, dims=NN):
    return lax.dot_general(a, b, dims, preferred_element_type=F32)


def layer_normalized(rows, axis=-1):
    average = jnp.mean(rows, axis, keepdims=True)
    centred = rows - average
    spread = jnp.mean(centred * centred, axis, keepdims=True)
    return centred * lax.rsqrt(spread + EPSILON)


def split_index(index, size):
    if size & (size - 1) == 0:
        return lax.shift_right_logical(index, jnp.int32(size.bit_length() - 1)), index & (size - 1)
    return lax.div(index, size), lax.rem(index, size)


def selection(size, source):
    row = lax.broadcasted_iota(jnp.int32, (size, size), 0)
    column = lax.broadcasted_iota(jnp.int32, (size, size), 1)
    return jnp.where(column == source(row), 1.0, 0.0).astype(BF16)


def head_mask(head, head_size, channels):
    lane = lax.broadcasted_iota(jnp.int32, (1, channels), 1)
    inside = (lane >= head * head_size) & (lane < (head + 1) * head_size)
    return jnp.where(inside, 1.0, 0.0).astype(BF16)


def fill(buffer, values):
    for k in range(buffer.shape[0]):
        buffer[k] = values[:, k * 128 : (k + 1) * 128]


def pick(buffer, start, size, stride):
    return jnp.concatenate(
        [buffer[k, pl.ds(start, size, stride=stride), :] for k in range(buffer.shape[0])], 1
    )


def landed(landing):
    blocks = landing[...].astype(F32)
    return blocks.reshape(blocks.shape[0] * blocks.shape[1], blocks.shape[2])


def softmax_rows(scores):
    top = jnp.max(scores, -1, keepdims=True)
    powers = jnp.exp(scores - top)
    return (powers / jnp.sum(powers, -1, keepdims=True)).astype(BF16)


def block_kernel(
    sizes,
    ids_h, mask_h, align_h, pair_h, table_h, bias_w_h, row_w_h, row_o_h, col_w_h, col_o_h,
    factor_w_h, outer_w_h, tri_w_h, tri_o_h,
    align_out_h, pair_out_h,
    ids, mask, align, pair, table, bias_w, row_w, row_o, col_w, col_o,
    factor_w, outer_w, tri_w, tri_o,
    bias_src, bias_land, msa_src, msa_land, right_src, right_land, tri_src, tri_land,
    back_src, back_land,
    bias_f, msa_f, outer_f, outer_w2, left_t, right_f, right_m, pair_one_v, tri_t, tri_f,
    land_f, comb_f, back_f, gate_v, align_v, pair_v,
    in_sem, out_sem, send_sem, recv_sem,
):
    count, seqs, rows, length, channels, heads, width, pair_chan, total = sizes
    own = pair_chan // count
    head_size = channels // heads
    me = lax.axis_index("res")
    barrier = pltpu.get_barrier_semaphore()

    @pl.loop(1, count)
    def _(step):
        pl.semaphore_signal(
            barrier, inc=1, device_id={"res": lax.rem(me + step, count)}, device_id_type=MESH
        )

    staged = [
        (pair_h, pair), (bias_w_h, bias_w), (align_h, align), (ids_h, ids), (table_h, table),
        (row_w_h, row_w), (mask_h, mask), (row_o_h, row_o), (col_w_h, col_w), (col_o_h, col_o),
        (factor_w_h, factor_w), (outer_w_h, outer_w), (tri_w_h, tri_w), (tri_o_h, tri_o),
    ]
    loads = [
        pltpu.make_async_copy(source, target, in_sem.at[k])
        for k, (source, target) in enumerate(staged)
    ]
    for load in loads:
        load.start()

    def send(number, source, landing, gather):
        @pl.loop(1, count)
        def _(step):
            peer = lax.rem(me + step, count)
            pltpu.make_async_remote_copy(
                src_ref=source if gather else source.at[peer],
                dst_ref=landing.at[me],
                send_sem=send_sem.at[number],
                recv_sem=recv_sem.at[number],
                device_id={"res": peer},
                device_id_type=MESH,
            ).start()

    def received(number, landing):
        others = landing.at[pl.ds(0, count - 1)]
        pltpu.make_async_copy(others, others, recv_sem.at[number]).wait()

    loads[0].wait()
    loads[1].wait()
    pieces = []
    for i in range(rows):
        normed = layer_normalized(pair[i].astype(F32)).astype(BF16)
        pieces.append(dot(bias_w[...], normed, (((0,), (1,)), ((), ()))))
    slab = jnp.concatenate(pieces, 0).astype(BF16)
    bias_src[...] = slab
    bias_land[me] = slab
    pl.semaphore_wait(barrier, count - 1)
    send(0, bias_src, bias_land, True)

    for load in loads[2:6]:
        load.wait()
    token = lax.broadcasted_iota(jnp.int32, (table.shape[0], length), 0)
    zero_rows = []
    for s in range(seqs):
        one_hot = jnp.where(ids[pl.ds(s, 1), :] == token, 1.0, 0.0).astype(BF16)
        zero_rows.append(align[s].astype(F32) + dot(one_hot, table[...], TN))
    msa_zero = jnp.concatenate(zero_rows, 0)
    projected = dot(layer_normalized(msa_zero).astype(BF16), row_w[...])
    masks = [head_mask(h, head_size, channels) for h in range(heads)]
    scale = head_size ** (-0.5)

    loads[6].wait()
    loads[7].wait()
    raw_scores, spread_values = [], []
    for s in range(seqs):
        part = projected[s * length : (s + 1) * length]
        query = (part[:, :channels] * scale).astype(BF16)
        key = part[:, channels : 2 * channels].astype(BF16)
        value = part[:, 2 * channels : 3 * channels].astype(BF16)
        stacked = jnp.concatenate([query * m for m in masks], 0)
        raw_scores.append(dot(stacked, key, NT))
        spread_values.append(jnp.concatenate([value * m for m in masks], 0))
    to_owner = selection(
        seqs * length,
        lambda o: (
            split_index(split_index(o, rows)[0], seqs)[1] * length
            + split_index(o, seqs * rows)[0] * rows
            + split_index(o, rows)[1]
        ),
    )
    for load in loads[8:]:
        load.wait()
    tri_t[...] = jnp.transpose(tri_w[:, : 4 * pair_chan].astype(F32), (1, 0)).astype(BF16)
    fill(outer_f, outer_w[...].astype(F32))
    for d in range(width):
        outer_w2[:, d * pair_chan : (d + 1) * pair_chan] = pick(
            outer_f, d, width, width
        ).astype(BF16)

    received(0, bias_land)
    fill(bias_f, landed(bias_land))
    mask_bias = (mask[...].astype(F32) - 1.0) * 10000.0
    extra = jnp.concatenate(
        [pick(bias_f, h, length, heads) for h in range(heads)], 0
    ) + mask_bias
    one_rows = []
    for s in range(seqs):
        weights = softmax_rows(raw_scores[s] + extra)
        side = jnp.concatenate(
            [weights[h * length : (h + 1) * length] for h in range(heads)], 1
        )
        mixed = dot(side, spread_values[s])
        gate = projected[s * length : (s + 1) * length, 3 * channels :]
        gated = (jax.nn.sigmoid(gate) * mixed).astype(BF16)
        zero = msa_zero[s * length : (s + 1) * length]
        one_rows.append((zero + dot(gated, row_o[...])).astype(BF16))
    ordered = dot(to_owner, jnp.concatenate(one_rows, 0))
    ordered = ordered.reshape(count, seqs * rows, channels)
    lane_parts = channels // 128
    slabs = jnp.concatenate(
        [ordered[:, :, k * 128 : (k + 1) * 128] for k in range(lane_parts)], 1
    ).astype(BF16)
    msa_src[...] = slabs
    msa_land[me] = msa_src[me]
    send(1, msa_src, msa_land, False)

    to_output = selection(
        total * rows,
        lambda o: (
            split_index(o, rows)[1] * total
            + split_index(split_index(o, rows)[0], seqs)[1] * count
            + split_index(o, seqs * rows)[0]
        ),
    )
    received(1, msa_land)
    fill(msa_f, landed(msa_land))
    step = lane_parts * seqs * rows
    column = jnp.concatenate(
        [
            jnp.concatenate(
                [
                    pick(msa_f, (k * seqs + s) * rows + i, count, step)
                    for i in range(rows)
                    for s in range(seqs)
                ],
                0,
            )
            for k in range(lane_parts)
        ],
        1,
    )
    projected = dot(layer_normalized(column).astype(BF16), col_w[...])
    gated_rows = []
    for i in range(rows):
        part = projected[i * total : (i + 1) * total]
        query = (part[:, :channels] * scale).astype(BF16)
        key = part[:, channels : 2 * channels].astype(BF16)
        value = part[:, 2 * channels : 3 * channels].astype(BF16)
        stacked = jnp.concatenate([query * m for m in masks], 0)
        weights = softmax_rows(dot(stacked, key, NT))
        every = dot(weights, value)
        mixed = every[:total] * masks[0].astype(F32)
        for h in range(1, heads):
            mixed = mixed + every[h * total : (h + 1) * total] * masks[h].astype(F32)
        gated_rows.append((jax.nn.sigmoid(part[:, 3 * channels :]) * mixed).astype(BF16))
    msa_two = column + dot(jnp.concatenate(gated_rows, 0), col_o[...])

    outer_input = layer_normalized(msa_two).astype(BF16)
    right_t = dot(factor_w[:, width:], outer_input, (((0,), (1,)), ((), ())))
    pack = max(1, 128 // total)
    groups = width // pack
    lanes = pack * total
    slabs = []
    if pack == 1:
        for i in range(rows):
            slabs.append(right_t[:, i * total : (i + 1) * total])
    else:
        lane = lax.broadcasted_iota(jnp.int32, (groups, lanes), 1)
        for i in range(rows):
            base, place = i // pack, i % pack
            joined = None
            for k in range(pack):
                piece = right_t[k * groups : (k + 1) * groups, base * lanes : (base + 1) * lanes]
                shift = ((k - place) * total) % lanes
                if shift:
                    piece = pltpu.roll(piece, shift, 1)
                joined = piece if joined is None else jnp.where(lane >= k * total, piece, joined)
            slabs.append(joined)
    slab = jnp.concatenate(slabs, 0).astype(BF16)
    right_src[...] = slab
    right_land[me] = slab
    send(2, right_src, right_land, True)

    ordered = dot(to_output, msa_two.astype(BF16)).astype(BF16)
    align_v[...] = ordered
    store_align = pltpu.make_async_copy(align_v, align_out_h, out_sem.at[0])
    store_align.start()
    left = dot(outer_input, factor_w[:, :width]).astype(BF16)
    chunk = 8
    for start in range(0, width, chunk):
        product = dot(left, outer_w2[:, start * pair_chan : (start + chunk) * pair_chan])
        for d in range(start, start + chunk):
            at = ((d % groups) * pack + d // groups) * total
            for i in range(rows):
                left_t[at : at + total, i * pair_chan : (i + 1) * pair_chan] = product[
                    i * total : (i + 1) * total,
                    (d - start) * pair_chan : (d - start + 1) * pair_chan,
                ].astype(BF16)

    received(2, right_land)
    fill(right_f, landed(right_land))
    for k in range(groups):
        right_m[:, k * lanes : (k + 1) * lanes] = pick(
            right_f, k, length, groups
        ).astype(BF16)
    update = dot(right_m[...], left_t[...]) * (1.0 / total)

    normed = []
    for i in range(rows):
        one = pair[i].astype(F32) + update[:, i * pair_chan : (i + 1) * pair_chan]
        pair_one_v[i] = one
        normed.append(layer_normalized(one).astype(BF16))
        factors = dot(tri_t[...], normed[i], NT)
        for k in range(2):
            low = 2 * k * pair_chan
            factor = (
                jax.nn.sigmoid(factors[low + pair_chan : low + 2 * pair_chan])
                * factors[low : low + pair_chan]
            )
            fill(tri_f.at[:, pl.ds((2 * i + k) * pair_chan, pair_chan), :], factor)
    for p in range(count):
        tri_src[p] = jnp.concatenate(
            [pick(tri_f, p * own + c, 2 * rows, pair_chan) for c in range(own)], 0
        ).astype(BF16)
    tri_land[me] = tri_src[me]
    send(3, tri_src, tri_land, False)

    for i in range(rows):
        gate_v[i] = jax.nn.sigmoid(dot(normed[i], tri_w[:, 4 * pair_chan :]))
    to_natural = selection(
        length, lambda o: split_index(o, rows)[1] * count + split_index(o, rows)[0]
    )

    received(3, tri_land)
    fill(land_f, landed(tri_land))
    stride = 2 * own * rows
    for c in range(own):
        sides = [
            jnp.concatenate(
                [
                    pick(land_f, (c * rows + i) * 2 + k, count, stride)
                    for i in range(rows)
                ],
                0,
            ).astype(BF16)
            for k in range(2)
        ]
        fill(comb_f.at[:, pl.ds(c * length, length), :], dot(sides[0], sides[1], NT))
    for p in range(count):
        back_src[p] = pick(comb_f, p, own * rows, count).astype(BF16)
    back_land[me] = back_src[me]
    send(4, back_src, back_land, False)

    received(4, back_land)
    fill(back_f, landed(back_land))
    for i in range(rows):
        combined = layer_normalized(pick(back_f, i, pair_chan, rows), 0).astype(BF16)
        turned = dot(to_natural, combined, NT).astype(BF16)
        result = pair_one_v[i] + gate_v[i] * dot(turned, tri_o[...])
        pair_v[i] = result.astype(BF16)
    store_pair = pltpu.make_async_copy(pair_v, pair_out_h, out_sem.at[1])
    store_pair.start()
    for number, landing in enumerate((bias_land, msa_land, right_land, tri_land, back_land)):
        others = landing.at[pl.ds(0, count - 1)]
        pltpu.make_async_copy(others, others, send_sem.at[number]).wait()
    store_align.wait()
    store_pair.wait()


def shards(
    homolog_symbol_ids,
    residue_attend_mask,
    alignment_state,
    pair,
    symbol_lookup_matrix,
    pair_bias_weight,
    row_projection_weight,
    horizontal_readout_matrix,
    column_projection_weight,
    vertical_readout_matrix,
    product_factor_matrices,
    outer_output_weight,
    triangle_input_weight,
    triangle_output_weight,
):
    count = lax.axis_size("res")
    seqs, length, channels = alignment_state.shape
    rows, _, pair_chan = pair.shape
    heads = pair_bias_weight.shape[1]
    width = product_factor_matrices.shape[1] // 2
    total = seqs * count
    own = pair_chan // count
    pack = max(1, 128 // total)
    groups, lanes = width // pack, pack * total
    operands = [
        homolog_symbol_ids,
        residue_attend_mask.reshape(1, length),
        alignment_state,
        pair,
        symbol_lookup_matrix,
        pair_bias_weight,
        row_projection_weight,
        horizontal_readout_matrix,
        column_projection_weight,
        vertical_readout_matrix,
        product_factor_matrices,
        outer_output_weight,
        triangle_input_weight,
        triangle_output_weight,
    ]
    lane_parts = channels // 128
    slab_rows = (
        (heads * rows, length),
        (lane_parts * seqs * rows, 128),
        (groups * rows, lanes),
        (2 * own * rows, length),
        (own * rows, length),
    )
    vmem = pltpu.VMEM
    exchanges = []
    for number, extent in enumerate(slab_rows):
        gathers = number in (0, 2)
        exchanges.append(vmem(extent if gathers else (count,) + extent, BF16))
        exchanges.append(vmem((count,) + extent, BF16))
    flat = [(b // 128, count * a, 128) for a, b in slab_rows]
    scratch = (
        [vmem(x.shape, x.dtype) for x in operands]
        + exchanges
        + [
            vmem(flat[0], F32),
            vmem(flat[1], F32),
            vmem((pair_chan // 128, width * width, 128), F32),
            vmem((width, width * pair_chan), BF16),
            vmem((width * total, rows * pair_chan), BF16),
            vmem(flat[2], F32),
            vmem((length, width * total), BF16),
            vmem(pair.shape, F32),
            vmem((4 * pair_chan, pair_chan), BF16),
            vmem((length // 128, 2 * rows * pair_chan, 128), F32),
            vmem(flat[3], F32),
            vmem((length // 128, own * length, 128), F32),
            vmem(flat[4], F32),
            vmem(pair.shape, F32),
            vmem((total * rows, channels), BF16),
            vmem(pair.shape, BF16),
            pltpu.SemaphoreType.DMA((len(operands),)),
            pltpu.SemaphoreType.DMA((2,)),
            pltpu.SemaphoreType.DMA((5,)),
            pltpu.SemaphoreType.DMA((5,)),
        ]
    )
    sizes = (count, seqs, rows, length, channels, heads, width, pair_chan, total)
    anywhere = pl.BlockSpec(memory_space=pl.ANY)
    alignment_output, pair_output = pl.pallas_call(
        functools.partial(block_kernel, sizes),
        out_shape=(
            jax.ShapeDtypeStruct((total * rows, channels), BF16),
            jax.ShapeDtypeStruct(pair.shape, BF16),
        ),
        in_specs=[anywhere] * len(operands),
        out_specs=(anywhere, anywhere),
        scratch_shapes=scratch,
        compiler_params=pltpu.CompilerParams(
            collective_id=0, has_side_effects=True, vmem_limit_bytes=60 * 1024 * 1024
        ),
    )(*operands)
    return (alignment_output.reshape(total, rows, channels), pair_output)


def solution(mesh):
    placed = (
        P(("crop", "res"), None),
        P("crop"),
        P(("crop", "res"), None, None),
        P(("crop", "res"), None, None),
        P(),
        P(),
        P(),
        P(),
        P(),
        P(),
        P(),
        P(),
        P(),
        P(),
    )
    return jax.shard_map(
        shards,
        mesh=mesh,
        in_specs=placed,
        out_specs=(P("crop", "res", None), P(("crop", "res"), None, None)),
        check_vma=False,
    )
```

time: 103 us -> 59.4 us (0.58)
  local copies, waits for them, and re-layouts: 20.9 us -> 4.43 us
  matrix products: 11.5 us -> 0 us
  Pallas kernels: 65.4 us -> 54.1 us
  other arithmetic: 3.39 us -> 0 us
    pallas_call x5 -> x1, Pallas kernels: 65.4 us -> 54.1 us  [shards(): pl.pallas_call(functools.partial(block_kernel, sizes), out_shape=(jax.Sha...]
    dot_general x17 -> x0, matrix products: 10.5 us -> none  [the longest x2 2.55 us: attention_block_fn(): jnp.einsum('bhqk,bkhd->bqhd', weights, value_tensor, preferred_element_ty...]
    reshape x8 -> x1, local copies, waits for them, and re-layouts: 7.14 us -> 1.63 us  [shards(): return (alignment_output.reshape(total, rows, channels), pair_output)]
    convert_element_type x9 -> x0, local copies, waits for them, and re-layouts: 4.9 us -> none  [the longest x1 1.04 us: shards(): back_rows.astype(jnp.float32)]
    slice x11 -> x0, local copies, waits for them, and re-layouts: 3.19 us -> none  [the longest x2 1.59 us: split_proj(): projected[..., 2 * channels:3 * channels].astype(jnp.bfloat16)]
    reduce_sum x10 -> x0, other arithmetic: 2.22 us -> none  [the longest x4 1.33 us: layer_normalized(): average = jnp.mean(input_rows, axis, keepdims=True)]
    unnamed x29 -> x7, local copies, waits for them, and re-layouts: 3.88 us -> 2.8 us
where the time goes in v1:
time: 59.4 us; the launch traced here: 59.2 us
  Pallas kernels  54.1 us (91%)
  local copies, waits for them, and re-layouts  4.43 us (7%)
  between operations  0.66 us (1%)
    pallas_call x1, Pallas kernels, shards(): pl.pallas_call(functools.partial(block_kernel, sizes), out_shape=(jax.Sha...  54.1 us
    unnamed x7, local copies, waits for them, and re-layouts  2.8 us
    reshape x1, local copies, waits for them, and re-layouts, shards(): return (alignment_output.reshape(total, rows, channels), pair_output)  1.63 us

profile of v1, /device:TPU:0, one launch (start us, length us, event | category | flops | bytes accessed | tf_op | source)
XLA Modules:
  0.0 59.2 jit_solution(2093118464194965378)
XLA Ops:
  0.6 0.0 copy-start.1
  0.6 1.4 %copy.16.bias_w_h = bf16[128,8]{1,0:T(8,128)(2,1)} copy(bf16[128,8]{0,1:T(8,128)(2,1)} %param.19) | data formatting | bytes 4096 | tf_op args[5]
  2.0 0.0 copy-done.1
  2.0 0.7 %copy.17.factor_w_h = bf16[256,64]{1,0:T(8,128)(2,1)} copy(bf16[256,64]{0,1:T(8,128)(2,1)S(1)} %copy-done.1) | data formatting | bytes 65536 | tf_op args[10]
  2.8 54.1 %shard_map.149 = (bf16[256,256]{1,0:T(8,128)(2,1)}, bf16[4,128,128]{2,1,0:T(8,128)(2,1)}) custom-call(s32[2,128]{1,0:T(2,128)} %ids_h.1, s32[1,128]{1,0:T(1,128)} %bitcast.1, bf16[2,128,256]{2,1,0:T(8,128)(2,1)} %align_h.1, bf16[4,128,128]{2,1,0:T(8,128)(2,1)} %pair_h.1, bf16[23,256]{1,0:T(8,128)(2,1)} %table_h.1, bf16[128,8]{1,0:T(8,128)(2,1)} %copy.16.bias_w_h, ...), custom_call_target="tpu_custom_call" | custom-call | tf_op jit(solution)/shard_map/pallas_call | solution.py:441
  56.9 0.0 copy-start
  56.9 1.6 %reshape.11 = bf16[64,4,256]{2,1,0:T(4,128)(2,1)} reshape(bf16[256,256]{1,0:T(8,128)(2,1)} %get-tuple-element.4) | data formatting | bytes 262144 | tf_op jit(solution)/shard_map/reshape | solution.py:454
  58.6 0.0 copy-done
  58.6 0.7 %copy.19 = bf16[4,128,128]{2,1,0:T(8,128)(2,1)} copy(bf16[4,128,128]{2,1,0:T(8,128)(2,1)S(1)} %copy-done) | data formatting | bytes 262144
Async XLA Ops:
  0.6 1.4 %copy-start.1 = (bf16[256,64]{0,1:T(8,128)(2,1)S(1)}, bf16[256,64]{0,1:T(8,128)(2,1)}, u32[]{:S(2)}) copy-start(bf16[256,64]{0,1:T(8,128)(2,1)} %param.24) | copy-start | bytes 98308
  56.9 1.6 %copy-start = (bf16[4,128,128]{2,1,0:T(8,128)(2,1)S(1)}, bf16[4,128,128]{2,1,0:T(8,128)(2,1)}, u32[]{:S(2)}) copy-start(bf16[4,128,128]{2,1,0:T(8,128)(2,1)} %get-tuple-element.9) | copy-start | bytes 393220

commit v2 on v1

v2 whole, which is shorter than its diff:
```python
import functools

import jax
import jax.numpy as jnp
from jax import lax
from jax.experimental import pallas as pl
from jax.experimental.pallas import tpu as pltpu
from jax.sharding import PartitionSpec as P

EPSILON = 1e-05
MESH = pl.DeviceIdType.MESH
F32 = jnp.float32
BF16 = jnp.bfloat16

NN = (((1,), (0,)), ((), ()))
NT = (((1,), (1,)), ((), ()))
TN = (((0,), (0,)), ((), ()))


def dot(a, b, dims=NN):
    return lax.dot_general(a, b, dims, preferred_element_type=F32)


def layer_normalized(rows, axis=-1):
    average = jnp.mean(rows, axis, keepdims=True)
    centred = rows - average
    spread = jnp.mean(centred * centred, axis, keepdims=True)
    return centred * lax.rsqrt(spread + EPSILON)


def split_index(index, size):
    if size & (size - 1) == 0:
        return lax.shift_right_logical(index, jnp.int32(size.bit_length() - 1)), index & (size - 1)
    return lax.div(index, size), lax.rem(index, size)


def selection(size, source):
    row = lax.broadcasted_iota(jnp.int32, (size, size), 0)
    column = lax.broadcasted_iota(jnp.int32, (size, size), 1)
    return jnp.where(column == source(row), 1.0, 0.0).astype(BF16)


def head_mask(head, head_size, channels):
    lane = lax.broadcasted_iota(jnp.int32, (1, channels), 1)
    inside = (lane >= head * head_size) & (lane < (head + 1) * head_size)
    return jnp.where(inside, 1.0, 0.0).astype(BF16)


def fill(buffer, values):
    for k in range(buffer.shape[0]):
        buffer[k] = values[:, k * 128 : (k + 1) * 128]


def pick(buffer, start, size, stride):
    return jnp.concatenate(
        [buffer[k, pl.ds(start, size, stride=stride), :] for k in range(buffer.shape[0])], 1
    )


def landed(landing):
    blocks = landing[...].astype(F32)
    return blocks.reshape(-1, blocks.shape[-1])


def by_group(blocks, groups):
    size = blocks[0].shape[0] // groups
    if size % 8 == 0:
        return jnp.concatenate([b.reshape(groups, size, b.shape[1]) for b in blocks], 1)
    return jnp.stack(
        [
            jnp.concatenate([b[g * size : (g + 1) * size] for b in blocks], 0)
            for g in range(groups)
        ],
        0,
    )


def softmax_rows(scores):
    top = jnp.max(scores, -1, keepdims=True)
    powers = jnp.exp(scores - top)
    return (powers / jnp.sum(powers, -1, keepdims=True)).astype(BF16)


def block_kernel(
    sizes,
    ids_h, mask_h, align_h, pair_h, table_h, bias_w_h, row_w_h, row_o_h, col_w_h, col_o_h,
    factor_w_h, outer_w_h, tri_w_h, tri_o_h,
    align_out, pair_out,
    ids, mask, align, pair, table, bias_w, row_w, row_o, col_w, col_o,
    factor_w, outer_w, tri_w, tri_o,
    bias_src, bias_land, msa_src, msa_land, right_src, right_land, tri_left, left_land,
    tri_right, tri_land, back_src, back_land,
    bias_f, msa_f, outer_f, outer_w2, left_t, right_f, right_m, pair_one_v, tri_t,
    land_f, left_f, comb_f, back_f, gate_v,
    in_sem, send_sem, recv_sem, bias_sem, right_sem,
):
    count, seqs, rows, length, channels, heads, width, pair_chan, total = sizes
    head_size = channels // heads
    me = lax.axis_index("res")
    barrier = pltpu.get_barrier_semaphore()

    @pl.loop(1, count)
    def _(step):
        pl.semaphore_signal(
            barrier, inc=1, device_id={"res": lax.rem(me + step, count)}, device_id_type=MESH
        )

    staged = [
        (pair_h, pair), (bias_w_h, bias_w), (align_h, align), (ids_h, ids), (table_h, table),
        (row_w_h, row_w), (mask_h, mask), (row_o_h, row_o), (col_w_h, col_w), (col_o_h, col_o),
        (factor_w_h, factor_w), (outer_w_h, outer_w), (tri_w_h, tri_w), (tri_o_h, tri_o),
    ]
    loads = [
        pltpu.make_async_copy(source, target, in_sem.at[k])
        for k, (source, target) in enumerate(staged)
    ]
    for load in loads:
        load.start()

    def remote(source, target, number, received_by, peer):
        pltpu.make_async_remote_copy(
            src_ref=source,
            dst_ref=target,
            send_sem=send_sem.at[number],
            recv_sem=received_by,
            device_id={"res": peer},
            device_id_type=MESH,
        ).start()

    def taken(landing, semaphore):
        pltpu.make_async_copy(landing, landing, semaphore).wait()

    chips = count // 2
    partner = me + 1 - 2 * lax.rem(me, 2)
    flips = [
        (1 - 2 * lax.rem(lax.div(me, 2 << j), 2)) * (2 << j) for j in range(chips.bit_length() - 1)
    ]
    others = [me + sum(flips[j] for j in range(len(flips)) if (k >> j) & 1) for k in range(1, chips)]

    def gather_start(number, arrivals, source, landing, part):
        for k in reversed(range(chips - 1)):
            remote(
                source, landing.at[(me,) + part], number, arrivals.at[part + (k,)], others[k]
            )
        remote(source, landing.at[(me,) + part], number, recv_sem.at[number], partner)

    def gather_relay(number, arrivals, landing, part):
        for k in range(chips - 1):
            block = landing.at[(others[k],) + part]
            taken(block, arrivals.at[part + (k,)])
            remote(block, block, number, recv_sem.at[number], partner)

    def gather_finish(number, landing):
        taken(landing.at[pl.ds(0, chips)], recv_sem.at[number])

    half = count // 2
    group, first = lax.rem(me, half), lax.div(me, half) * half

    def spread(number, source, landing, size):
        @pl.loop(1, size)
        def _(step):
            if size == count:
                peer = lax.rem(me + step, count)
            else:
                peer = first + lax.rem(group + step, size)
            remote(source(peer), landing, number, recv_sem.at[number], peer)

    loads[0].wait()
    loads[1].wait()
    pieces = []
    for i in range(rows):
        normed = layer_normalized(pair[i].astype(F32)).astype(BF16)
        pieces.append(dot(bias_w[...], normed, NT))
    slab = jnp.concatenate(pieces, 0).astype(BF16)
    bias_src[...] = slab
    bias_land[me] = slab
    pl.semaphore_wait(barrier, count - 1)
    gather_start(0, bias_sem, bias_src, bias_land, ())

    for load in loads[2:6]:
        load.wait()
    token = lax.broadcasted_iota(jnp.int32, (table.shape[0], length), 0)
    zero_rows = []
    for s in range(seqs):
        one_hot = jnp.where(ids[pl.ds(s, 1), :] == token, 1.0, 0.0).astype(BF16)
        zero_rows.append(align[s].astype(F32) + dot(one_hot, table[...], TN))
    msa_zero = jnp.concatenate(zero_rows, 0)
    projected = dot(layer_normalized(msa_zero).astype(BF16), row_w[...])
    masks = [head_mask(h, head_size, channels) for h in range(heads)]
    scale = head_size ** (-0.5)

    loads[6].wait()
    loads[7].wait()
    raw_scores, spread_values = [], []
    for s in range(seqs):
        part = projected[s * length : (s + 1) * length]
        query = (part[:, :channels] * scale).astype(BF16)
        key = part[:, channels : 2 * channels].astype(BF16)
        value = part[:, 2 * channels : 3 * channels].astype(BF16)
        stacked = jnp.concatenate([query * m for m in masks], 0)
        raw_scores.append(dot(stacked, key, NT))
        spread_values.append(jnp.concatenate([value * m for m in masks], 0))
    to_owner = selection(
        seqs * length,
        lambda o: (
            split_index(split_index(o, rows)[0], seqs)[1] * length
            + split_index(o, seqs * rows)[0] * rows
            + split_index(o, rows)[1]
        ),
    )
    for load in loads[8:]:
        load.wait()
    tri_t[...] = jnp.transpose(tri_w[:, : 4 * pair_chan].astype(F32), (1, 0)).astype(BF16)
    fill(outer_f, outer_w[...].astype(F32))
    for d in range(width):
        outer_w2[:, d * pair_chan : (d + 1) * pair_chan] = pick(
            outer_f, d, width, width
        ).astype(BF16)

    gather_relay(0, bias_sem, bias_land, ())
    gather_finish(0, bias_land)
    fill(bias_f, landed(bias_land))
    mask_bias = (mask[...].astype(F32) - 1.0) * 10000.0
    extra = jnp.concatenate(
        [pick(bias_f, h, length, heads) for h in range(heads)], 0
    ) + mask_bias
    one_rows = []
    for s in range(seqs):
        weights = softmax_rows(raw_scores[s] + extra)
        side = jnp.concatenate(
            [weights[h * length : (h + 1) * length] for h in range(heads)], 1
        )
        mixed = dot(side, spread_values[s])
        gate = projected[s * length : (s + 1) * length, 3 * channels :]
        gated = (jax.nn.sigmoid(gate) * mixed).astype(BF16)
        zero = msa_zero[s * length : (s + 1) * length]
        one_rows.append((zero + dot(gated, row_o[...])).astype(BF16))
    ordered = dot(to_owner, jnp.concatenate(one_rows, 0))
    ordered = ordered.reshape(count, seqs * rows, channels)
    lane_parts = channels // 128
    slabs = jnp.concatenate(
        [ordered[:, :, k * 128 : (k + 1) * 128] for k in range(lane_parts)], 1
    ).astype(BF16)
    msa_src[...] = slabs
    msa_land[me] = msa_src[me]
    spread(1, lambda peer: msa_src.at[peer], msa_land.at[me], count)

    to_output = selection(
        total * rows,
        lambda o: (
            split_index(o, rows)[1] * total
            + split_index(split_index(o, rows)[0], seqs)[1] * count
            + split_index(o, seqs * rows)[0]
        ),
    )
    taken(msa_land.at[pl.ds(0, count - 1)], recv_sem.at[1])
    fill(msa_f, landed(msa_land))
    step = lane_parts * seqs * rows
    column = jnp.concatenate(
        [
            jnp.concatenate(
                [
                    pick(msa_f, (k * seqs + s) * rows + i, count, step)
                    for i in range(rows)
                    for s in range(seqs)
                ],
                0,
            )
            for k in range(lane_parts)
        ],
        1,
    )
    pack = max(1, 128 // total)
    groups = width // pack
    lanes = pack * total
    lane = lax.broadcasted_iota(jnp.int32, (groups, lanes), 1)
    two_rows, inputs = [], []
    for start in range(0, rows, pack):
        block = column[start * total : (start + pack) * total]
        projected = dot(layer_normalized(block).astype(BF16), col_w[...])
        gated_rows = []
        for i in range(pack):
            part = projected[i * total : (i + 1) * total]
            query = (part[:, :channels] * scale).astype(BF16)
            key = part[:, channels : 2 * channels].astype(BF16)
            value = part[:, 2 * channels : 3 * channels].astype(BF16)
            stacked = jnp.concatenate([query * m for m in masks], 0)
            weights = softmax_rows(dot(stacked, key, NT))
            every = dot(weights, value)
            mixed = every[:total] * masks[0].astype(F32)
            for h in range(1, heads):
                mixed = mixed + every[h * total : (h + 1) * total] * masks[h].astype(F32)
            gated_rows.append((jax.nn.sigmoid(part[:, 3 * channels :]) * mixed).astype(BF16))
        msa_two = block + dot(jnp.concatenate(gated_rows, 0), col_o[...])
        outer_input = layer_normalized(msa_two).astype(BF16)
        two_rows.append(msa_two.astype(BF16))
        inputs.append(outer_input)

        right_t = dot(factor_w[width:, :], outer_input, NT)
        slabs = []
        for place in range(pack):
            joined = None
            for k in range(pack):
                piece = right_t[k * groups : (k + 1) * groups]
                shift = ((k - place) * total) % lanes
                if shift:
                    piece = pltpu.roll(piece, shift, 1)
                joined = piece if joined is None else jnp.where(lane >= k * total, piece, joined)
            slabs.append(joined)
        slab = jnp.concatenate(slabs, 0).astype(BF16)
        part = (start // pack,)
        right_src[part[0]] = slab
        right_land[me, part[0]] = slab
        gather_start(2, right_sem, right_src.at[part[0]], right_land, part)

    ordered = dot(to_output, jnp.concatenate(two_rows, 0))
    align_out[...] = ordered.reshape(total, rows, channels).astype(BF16)
    left = dot(jnp.concatenate(inputs, 0), factor_w[:width, :], NT).astype(BF16)
    chunk = 8
    for start in range(0, width, chunk):
        product = dot(left, outer_w2[:, start * pair_chan : (start + chunk) * pair_chan])
        for d in range(start, start + chunk):
            at = ((d % groups) * pack + d // groups) * total
            for i in range(rows):
                left_t[at : at + total, i * pair_chan : (i + 1) * pair_chan] = product[
                    i * total : (i + 1) * total,
                    (d - start) * pair_chan : (d - start + 1) * pair_chan,
                ].astype(BF16)

    for k in range(rows // pack):
        gather_relay(2, right_sem, right_land, (k,))
    gather_finish(2, right_land)
    fill(right_f, landed(right_land))
    for k in range(groups):
        right_m[:, k * lanes : (k + 1) * lanes] = pick(right_f, k, length, groups).astype(BF16)

    own = pair_chan // half
    normed = []
    pairs = tri_left.shape[0]
    pair_rows = rows // pairs
    for q in range(pairs):
        columns = pl.ds(q * pair_rows * pair_chan, pair_rows * pair_chan)
        update = dot(right_m[...], left_t[:, columns]) * (1.0 / total)
        sides = [[], []]
        for k in range(pair_rows):
            i = q * pair_rows + k
            one = pair[i].astype(F32) + update[:, k * pair_chan : (k + 1) * pair_chan]
            pair_one_v[i] = one
            normed.append(layer_normalized(one).astype(BF16))
            factors = dot(tri_t[...], normed[i], NT)
            for side in range(2):
                low = 2 * side * pair_chan
                sides[side].append(
                    jax.nn.sigmoid(factors[low + pair_chan : low + 2 * pair_chan])
                    * factors[low : low + pair_chan]
                )
        tri_left[q] = by_group(sides[0], half).astype(BF16)
        tri_right[q] = by_group(sides[1], half).astype(BF16)
        left_land[group, q] = tri_left[q, group]
        tri_land[me, q] = tri_right[q, group]
        spread(
            3, lambda peer: tri_right.at[q, lax.rem(peer, half)], tri_land.at[me, q], count
        )
        spread(4, lambda peer: tri_left.at[q, lax.rem(peer, half)], left_land.at[group, q], half)

    for i in range(rows):
        gate_v[i] = jax.nn.sigmoid(dot(normed[i], tri_w[:, 4 * pair_chan :]))
    taken(tri_land.at[pl.ds(0, count - 1)], recv_sem.at[3])
    taken(left_land.at[pl.ds(0, half - 1)], recv_sem.at[4])
    fill(land_f, landed(tri_land))
    fill(left_f, landed(left_land))
    block = half * rows
    for c in range(own):
        left_side = jnp.concatenate(
            [pick(left_f, i * own + c, half, own * rows) for i in range(rows)], 0
        ).astype(BF16)
        right_side = pick(land_f, c, length, own).astype(BF16)
        fill(comb_f.at[:, pl.ds(c * block, block), :], dot(left_side, right_side, NT))
    for p in range(half):
        back_src[p] = pick(comb_f, p, own * rows, half).astype(BF16)
    back_land[group] = back_src[group]
    spread(5, lambda peer: back_src.at[lax.rem(peer, half)], back_land.at[group], half)

    taken(back_land.at[pl.ds(0, half - 1)], recv_sem.at[5])
    fill(back_f, landed(back_land))
    for i in range(rows):
        combined = layer_normalized(pick(back_f, i, pair_chan, rows), 0).astype(BF16)
        result = pair_one_v[i] + gate_v[i] * dot(combined, tri_o[...], TN)
        pair_out[i] = result.astype(BF16)
    for number, sent in enumerate((bias_land, msa_land, right_land, tri_land)):
        taken(sent.at[pl.ds(0, count - 1)], send_sem.at[number])
    taken(left_land.at[pl.ds(0, half - 1)], send_sem.at[4])
    taken(back_land.at[pl.ds(0, half - 1)], send_sem.at[5])


def shards(
    homolog_symbol_ids,
    residue_attend_mask,
    alignment_state,
    pair,
    symbol_lookup_matrix,
    pair_bias_weight,
    row_projection_weight,
    horizontal_readout_matrix,
    column_projection_weight,
    vertical_readout_matrix,
    product_factor_matrices,
    outer_output_weight,
    triangle_input_weight,
    triangle_output_weight,
):
    count = lax.axis_size("res")
    seqs, length, channels = alignment_state.shape
    rows, _, pair_chan = pair.shape
    heads = pair_bias_weight.shape[1]
    width = product_factor_matrices.shape[1] // 2
    total = seqs * count
    half = count // 2
    own = pair_chan // half
    pack = max(1, 128 // total)
    groups, lanes = width // pack, pack * total
    operands = [
        homolog_symbol_ids,
        residue_attend_mask.reshape(1, length),
        alignment_state,
        pair,
        symbol_lookup_matrix,
        pair_bias_weight.T,
        row_projection_weight,
        horizontal_readout_matrix,
        column_projection_weight,
        vertical_readout_matrix,
        product_factor_matrices.T,
        outer_output_weight,
        triangle_input_weight,
        triangle_output_weight,
    ]
    lane_parts = channels // 128
    vmem = pltpu.VMEM
    parts, pairs = rows // pack, 2
    tri_slab = (pairs, half, own * rows // pairs, length)
    exchanges = [
        vmem((heads * rows, length), BF16),
        vmem((count, heads * rows, length), BF16),
        vmem((count, lane_parts * seqs * rows, 128), BF16),
        vmem((count, lane_parts * seqs * rows, 128), BF16),
        vmem((parts, groups * pack, lanes), BF16),
        vmem((count, parts, groups * pack, lanes), BF16),
        vmem(tri_slab, BF16),
        vmem((half, pairs) + tri_slab[2:], BF16),
        vmem(tri_slab, BF16),
        vmem((count, pairs) + tri_slab[2:], BF16),
        vmem((half, own * rows, length), BF16),
        vmem((half, own * rows, length), BF16),
    ]

    def pieces(row_count, lane_count):
        return vmem((lane_count // 128, row_count, 128), F32)

    scratch = (
        [vmem(x.shape, x.dtype) for x in operands]
        + exchanges
        + [
            pieces(count * heads * rows, length),
            pieces(count * lane_parts * seqs * rows, 128),
            pieces(width * width, pair_chan),
            vmem((width, width * pair_chan), BF16),
            vmem((width * total, rows * pair_chan), BF16),
            pieces(length * groups, lanes),
            vmem((length, width * total), BF16),
            vmem(pair.shape, F32),
            vmem((4 * pair_chan, pair_chan), BF16),
            pieces(count * own * rows, length),
            pieces(half * own * rows, length),
            pieces(half * own * rows, length),
            pieces(half * own * rows, length),
            vmem(pair.shape, F32),
            pltpu.SemaphoreType.DMA((len(operands),)),
            pltpu.SemaphoreType.DMA((6,)),
            pltpu.SemaphoreType.DMA((6,)),
            pltpu.SemaphoreType.DMA((half - 1,)),
            pltpu.SemaphoreType.DMA((parts, half - 1)),
        ]
    )
    sizes = (count, seqs, rows, length, channels, heads, width, pair_chan, total)
    anywhere = pl.BlockSpec(memory_space=pl.ANY)
    inside = pl.BlockSpec(memory_space=pltpu.VMEM)
    alignment_output, pair_output = pl.pallas_call(
        functools.partial(block_kernel, sizes),
        out_shape=(
            jax.ShapeDtypeStruct((total, rows, channels), BF16),
            jax.ShapeDtypeStruct(pair.shape, BF16),
        ),
        in_specs=[anywhere] * len(operands),
        out_specs=(inside, inside),
        scratch_shapes=scratch,
        compiler_params=pltpu.CompilerParams(
            collective_id=0, has_side_effects=True, vmem_limit_bytes=60 * 1024 * 1024
        ),
    )(*operands)
    return (alignment_output, pair_output)


def solution(mesh):
    placed = (
        P(("crop", "res"), None),
        P("crop"),
        P(("crop", "res"), None, None),
        P(("crop", "res"), None, None),
        P(),
        P(),
        P(),
        P(),
        P(),
        P(),
        P(),
        P(),
        P(),
        P(),
    )
    return jax.shard_map(
        shards,
        mesh=mesh,
        in_specs=placed,
        out_specs=(P("crop", "res", None), P(("crop", "res"), None, None)),
        check_vma=False,
    )
```

time: 59.4 us -> 49 us (0.82)
  Pallas kernels: 54.1 us -> 45.9 us
  local copies, waits for them, and re-layouts: 4.43 us -> 2.3 us
    pallas_call x1, Pallas kernels: 54.1 us -> 45.9 us  [shards(): pl.pallas_call(functools.partial(block_kernel, sizes), out_shape=(jax.Sha...]
    reshape x1 -> x0, local copies, waits for them, and re-layouts: 1.63 us -> none  [shards(): return (alignment_output.reshape(total, rows, channels), pair_output)]
    unnamed x7 -> x4, local copies, waits for them, and re-layouts: 2.8 us -> 2.3 us
where the time goes in v2:
time: 49 us; the launch traced here: 48.8 us
  Pallas kernels  45.9 us (94%)
  local copies, waits for them, and re-layouts  2.3 us (5%)
  between operations  0.65 us (1%)
    pallas_call x1, Pallas kernels, shards(): pl.pallas_call(functools.partial(block_kernel, sizes), out_shape=(jax.Sha...  45.9 us
    unnamed x4, local copies, waits for them, and re-layouts  2.3 us

profile of v2, /device:TPU:0, one launch (start us, length us, event | category | flops | bytes accessed | tf_op | source)
XLA Modules:
  0.0 48.8 jit_solution(5921170288797502170)
XLA Ops:
  0.6 45.9 %shard_map.149 = (bf16[64,4,256]{2,1,0:T(4,128)(2,1)}, bf16[4,128,128]{2,1,0:T(8,128)(2,1)}) custom-call(s32[2,128]{1,0:T(2,128)} %ids_h.1, s32[1,128]{1,0:T(1,128)} %bitcast.5, bf16[2,128,256]{2,1,0:T(8,128)(2,1)} %align_h.1, bf16[4,128,128]{2,1,0:T(8,128)(2,1)} %pair_h.1, bf16[23,256]{1,0:T(8,128)(2,1)} %table_h.1, bf16[8,128]{1,0:T(8,128)(2,1)} %bitcast.4, ...), custom_call_target="tpu_custom_call" | custom-call | tf_op jit(solution)/shard_map/pallas_call | solution.py:488
  46.5 0.0 copy-start
  46.5 1.6 %copy.18 = bf16[64,4,256]{2,1,0:T(4,128)(2,1)} copy(bf16[64,4,256]{2,1,0:T(4,128)(2,1)} %get-tuple-element.4) | data formatting | bytes 262144
  48.2 0.0 copy-done
  48.2 0.7 %copy.19 = bf16[4,128,128]{2,1,0:T(8,128)(2,1)} copy(bf16[4,128,128]{2,1,0:T(8,128)(2,1)S(1)} %copy-done) | data formatting | bytes 262144
Async XLA Ops:
  46.5 1.7 %copy-start = (bf16[4,128,128]{2,1,0:T(8,128)(2,1)S(1)}, bf16[4,128,128]{2,1,0:T(8,128)(2,1)}, u32[]{:S(2)}) copy-start(bf16[4,128,128]{2,1,0:T(8,128)(2,1)} %get-tuple-element.5) | copy-start | bytes 393220

commit v3 on v2

--- a/solution.py
+++ b/solution.py
@@ -9,6 +9,7 @@
 
 EPSILON = 1e-05
 MESH = pl.DeviceIdType.MESH
+VMEM_BYTES = 40 * 1024 * 1024
 F32 = jnp.float32
 BF16 = jnp.bfloat16
 
@@ -84,14 +85,14 @@
 def block_kernel(
     sizes,
     ids_h, mask_h, align_h, pair_h, table_h, bias_w_h, row_w_h, row_o_h, col_w_h, col_o_h,
-    factor_w_h, outer_w_h, tri_w_h, tri_o_h,
-    align_out, pair_out,
+    factor_w_h, outer_w_h, tri_w_h,
+    align_out, back_land, pair_one_v, gate_v,
     ids, mask, align, pair, table, bias_w, row_w, row_o, col_w, col_o,
-    factor_w, outer_w, tri_w, tri_o,
+    factor_w, outer_w, tri_w,
     bias_src, bias_land, msa_src, msa_land, right_src, right_land, tri_left, left_land,
-    tri_right, tri_land, back_src, back_land,
-    bias_f, msa_f, outer_f, outer_w2, left_t, right_f, right_m, pair_one_v, tri_t,
-    land_f, left_f, comb_f, back_f, gate_v,
+    tri_right, tri_land, back_src,
+    bias_f, msa_f, outer_f, outer_w2, left_t, right_f, right_m, tri_t,
+    land_f, left_f, comb_f,
     in_sem, send_sem, recv_sem, bias_sem, right_sem,
 ):
     count, seqs, rows, length, channels, heads, width, pair_chan, total = sizes
@@ -108,7 +109,7 @@
     staged = [
         (pair_h, pair), (bias_w_h, bias_w), (align_h, align), (ids_h, ids), (table_h, table),
         (row_w_h, row_w), (mask_h, mask), (row_o_h, row_o), (col_w_h, col_w), (col_o_h, col_o),
-        (factor_w_h, factor_w), (outer_w_h, outer_w), (tri_w_h, tri_w), (tri_o_h, tri_o),
+        (factor_w_h, factor_w), (outer_w_h, outer_w), (tri_w_h, tri_w),
     ]
     loads = [
         pltpu.make_async_copy(source, target, in_sem.at[k])
@@ -313,8 +314,6 @@
         right_land[me, part[0]] = slab
         gather_start(2, right_sem, right_src.at[part[0]], right_land, part)
 
-    ordered = dot(to_output, jnp.concatenate(two_rows, 0))
-    align_out[...] = ordered.reshape(total, rows, channels).astype(BF16)
     left = dot(jnp.concatenate(inputs, 0), factor_w[:width, :], NT).astype(BF16)
     chunk = 8
     for start in range(0, width, chunk):
@@ -363,6 +362,8 @@
         )
         spread(4, lambda peer: tri_left.at[q, lax.rem(peer, half)], left_land.at[group, q], half)
 
+    ordered = dot(to_output, jnp.concatenate(two_rows, 0))
+    align_out[...] = ordered.reshape(total, rows, channels).astype(BF16)
     for i in range(rows):
         gate_v[i] = jax.nn.sigmoid(dot(normed[i], tri_w[:, 4 * pair_chan :]))
     taken(tri_land.at[pl.ds(0, count - 1)], recv_sem.at[3])
@@ -382,15 +383,24 @@
     spread(5, lambda peer: back_src.at[lax.rem(peer, half)], back_land.at[group], half)
 
     taken(back_land.at[pl.ds(0, half - 1)], recv_sem.at[5])
-    fill(back_f, landed(back_land))
-    for i in range(rows):
-        combined = layer_normalized(pick(back_f, i, pair_chan, rows), 0).astype(BF16)
-        result = pair_one_v[i] + gate_v[i] * dot(combined, tri_o[...], TN)
-        pair_out[i] = result.astype(BF16)
     for number, sent in enumerate((bias_land, msa_land, right_land, tri_land)):
         taken(sent.at[pl.ds(0, count - 1)], send_sem.at[number])
     taken(left_land.at[pl.ds(0, half - 1)], send_sem.at[4])
     taken(back_land.at[pl.ds(0, half - 1)], send_sem.at[5])
+
+
+def finish_kernel(rows, align, back_land, pair_one, gate, tri_o, align_out, pair_out, back_f, pair_v, sem):
+    store_align = pltpu.make_async_copy(align, align_out, sem.at[0])
+    store_align.start()
+    fill(back_f, landed(back_land))
+    for i in range(rows):
+        combined = layer_normalized(pick(back_f, i, pair_one.shape[2], rows), 0).astype(BF16)
+        result = pair_one[i] + gate[i] * dot(combined, tri_o[...], TN)
+        pair_v[i] = result.astype(BF16)
+    store_pair = pltpu.make_async_copy(pair_v, pair_out, sem.at[1])
+    store_pair.start()
+    store_align.wait()
+    store_pair.wait()
 
 
 def shards(
@@ -433,7 +443,6 @@
         product_factor_matrices.T,
         outer_output_weight,
         triangle_input_weight,
-        triangle_output_weight,
     ]
     lane_parts = channels // 128
     vmem = pltpu.VMEM
@@ -451,7 +460,6 @@
         vmem(tri_slab, BF16),
         vmem((count, pairs) + tri_slab[2:], BF16),
         vmem((half, own * rows, length), BF16),
-        vmem((half, own * rows, length), BF16),
     ]
 
     def pieces(row_count, lane_count):
@@ -468,13 +476,10 @@
             vmem((width * total, rows * pair_chan), BF16),
             pieces(length * groups, lanes),
             vmem((length, width * total), BF16),
-            vmem(pair.shape, F32),
             vmem((4 * pair_chan, pair_chan), BF16),
             pieces(count * own * rows, length),
             pieces(half * own * rows, length),
             pieces(half * own * rows, length),
-            pieces(half * own * rows, length),
-            vmem(pair.shape, F32),
             pltpu.SemaphoreType.DMA((len(operands),)),
             pltpu.SemaphoreType.DMA((6,)),
             pltpu.SemaphoreType.DMA((6,)),
@@ -483,22 +488,38 @@
         ]
     )
     sizes = (count, seqs, rows, length, channels, heads, width, pair_chan, total)
-    anywhere = pl.BlockSpec(memory_space=pl.ANY)
+    anywhere = pl.BlockSpec(memory_space=pltpu.HBM)
     inside = pl.BlockSpec(memory_space=pltpu.VMEM)
-    alignment_output, pair_output = pl.pallas_call(
+    aligned, back, pair_one, gate = pl.pallas_call(
         functools.partial(block_kernel, sizes),
+        out_shape=(
+            jax.ShapeDtypeStruct((total, rows, channels), BF16),
+            jax.ShapeDtypeStruct((half, own * rows, length), BF16),
+            jax.ShapeDtypeStruct(pair.shape, F32),
+            jax.ShapeDtypeStruct(pair.shape, F32),
+        ),
+        in_specs=[anywhere] * len(operands),
+        out_specs=(inside,) * 4,
+        scratch_shapes=scratch,
+        compiler_params=pltpu.CompilerParams(
+            collective_id=0, has_side_effects=True, vmem_limit_bytes=VMEM_BYTES
+        ),
+    )(*[pltpu.with_memory_space_constraint(x, pltpu.HBM) for x in operands])
+    return pl.pallas_call(
+        functools.partial(finish_kernel, rows),
         out_shape=(
             jax.ShapeDtypeStruct((total, rows, channels), BF16),
             jax.ShapeDtypeStruct(pair.shape, BF16),
         ),
-        in_specs=[anywhere] * len(operands),
-        out_specs=(inside, inside),
-        scratch_shapes=scratch,
-        compiler_params=pltpu.CompilerParams(
-            collective_id=0, has_side_effects=True, vmem_limit_bytes=60 * 1024 * 1024
-        ),
-    )(*operands)
-    return (alignment_output, pair_output)
+        in_specs=[inside] * 5,
+        out_specs=(anywhere, anywhere),
+        scratch_shapes=[
+            pieces(half * own * rows, length),
+            vmem(pair.shape, BF16),
+            pltpu.SemaphoreType.DMA((2,)),
+        ],
+        compiler_params=pltpu.CompilerParams(vmem_limit_bytes=VMEM_BYTES // 4),
+    )(aligned, back, pair_one, gate, triangle_output_weight)
 
 
 def solution(mesh):

time: 49 us -> 46.7 us (0.953)
  local copies, waits for them, and re-layouts: 2.3 us -> 0.01 us
    unnamed x4 -> x2, local copies, waits for them, and re-layouts: 2.3 us -> 0.01 us
    pallas_call x1, Pallas kernels: 45.9 us -> 44.9 us  [shards(): pl.pallas_call(functools.partial(block_kernel, sizes), out_shape=(jax.Sha...]
    pallas_call x0 -> x1, Pallas kernels: none -> 0.98 us  [shards(): pl.pallas_call(functools.partial(finish_kernel, rows), out_shape=(jax.Sha...]
where the time goes in v3:
time: 46.7 us; the launch traced here: 46.5 us
  Pallas kernels  45.9 us (98%)
  between operations  0.66 us (1%)
    pallas_call x1, Pallas kernels, shards(): pl.pallas_call(functools.partial(block_kernel, sizes), out_shape=(jax.Sha...  44.9 us
    pallas_call x1, Pallas kernels, shards(): pl.pallas_call(functools.partial(finish_kernel, rows), out_shape=(jax.Sha...  0.98 us

profile of v3, /device:TPU:0, one launch (start us, length us, event | category | flops | bytes accessed | tf_op | source)
XLA Modules:
  0.0 46.5 jit_solution(11434499978434960743)
XLA Ops:
  0.6 0.0 copy-start
  0.6 44.9 %shard_map.149 = (bf16[64,4,256]{2,1,0:T(4,128)(2,1)S(1)}, bf16[16,32,128]{2,1,0:T(8,128)(2,1)S(1)}, f32[4,128,128]{2,1,0:T(8,128)S(1)}, f32[4,128,128]{2,1,0:T(8,128)S(1)}) custom-call(s32[2,128]{1,0:T(2,128)} %ids_h.1, s32[1,128]{1,0:T(1,128)} %bitcast.5, bf16[2,128,256]{2,1,0:T(8,128)(2,1)} %align_h.1, bf16[4,128,128]{2,1,0:T(8,128)(2,1)} %pair_h.1, ...), custom_call_target="tpu_custom_call" | custom-call | tf_op jit(solution)/shard_map/pallas_call | solution.py:493
  45.5 0.0 copy-done
  45.5 1.0 %shard_map.150 = (bf16[64,4,256]{2,1,0:T(4,128)(2,1)}, bf16[4,128,128]{2,1,0:T(8,128)(2,1)}) custom-call(bf16[64,4,256]{2,1,0:T(4,128)(2,1)S(1)} %get-tuple-element.6.align, bf16[16,32,128]{2,1,0:T(8,128)(2,1)S(1)} %get-tuple-element.7.back_land, f32[4,128,128]{2,1,0:T(8,128)S(1)} %get-tuple-element.8.pair_one, f32[4,128,128]{2,1,0:T(8,128)S(1)} %get-tuple-element.9.gate, ...), custom_call_target="tpu_custom_call" | custom-call | tf_op jit(solution)/shard_map/pallas_call | solution.py:508
Async XLA Ops:
  0.6 44.9 %copy-start = (bf16[128,128]{1,0:T(8,128)(2,1)S(1)}, bf16[128,128]{1,0:T(8,128)(2,1)}, u32[]{:S(2)}) copy-start(bf16[128,128]{1,0:T(8,128)(2,1)} %tri_o.1) | copy-start | bytes 98308

commit v4 on v3

--- a/solution.py
+++ b/solution.py
@@ -63,17 +63,22 @@
     return blocks.reshape(-1, blocks.shape[-1])
 
 
-def by_group(blocks, groups):
-    size = blocks[0].shape[0] // groups
-    if size % 8 == 0:
-        return jnp.concatenate([b.reshape(groups, size, b.shape[1]) for b in blocks], 1)
-    return jnp.stack(
-        [
-            jnp.concatenate([b[g * size : (g + 1) * size] for b in blocks], 0)
-            for g in range(groups)
-        ],
-        0,
-    )
+def pack_lanes(block, pack, size):
+    if pack == 1:
+        return [block]
+    height, lanes = block.shape[0] // pack, pack * size
+    lane = lax.broadcasted_iota(jnp.int32, (height, lanes), 1)
+    packed = []
+    for place in range(pack):
+        joined = None
+        for k in range(pack):
+            piece = block[k * height : (k + 1) * height]
+            shift = ((k - place) * size) % lanes
+            if shift:
+                piece = pltpu.roll(piece, shift, 1)
+            joined = piece if joined is None else jnp.where(lane >= k * size, piece, joined)
+        packed.append(joined)
+    return packed
 
 
 def softmax_rows(scores):
@@ -92,7 +97,7 @@
     bias_src, bias_land, msa_src, msa_land, right_src, right_land, tri_left, left_land,
     tri_right, tri_land, back_src,
     bias_f, msa_f, outer_f, outer_w2, left_t, right_f, right_m, tri_t,
-    land_f, left_f, comb_f,
+    tri_f, land_f, left_f, comb_f,
     in_sem, send_sem, recv_sem, bias_sem, right_sem,
 ):
     count, seqs, rows, length, channels, heads, width, pair_chan, total = sizes
@@ -145,14 +150,14 @@
             )
         remote(source, landing.at[(me,) + part], number, recv_sem.at[number], partner)
 
-    def gather_relay(number, arrivals, landing, part):
-        for k in range(chips - 1):
+    def gather_relay(number, arrivals, landing, part, steps, handed):
+        for k in steps:
             block = landing.at[(others[k],) + part]
             taken(block, arrivals.at[part + (k,)])
-            remote(block, block, number, recv_sem.at[number], partner)
-
-    def gather_finish(number, landing):
-        taken(landing.at[pl.ds(0, chips)], recv_sem.at[number])
+            remote(block, block, number, recv_sem.at[handed], partner)
+
+    def gather_finish(handed, landing, blocks):
+        taken(landing.at[pl.ds(0, blocks)], recv_sem.at[handed])
 
     half = count // 2
     group, first = lax.rem(me, half), lax.div(me, half) * half
@@ -218,8 +223,8 @@
             outer_f, d, width, width
         ).astype(BF16)
 
-    gather_relay(0, bias_sem, bias_land, ())
-    gather_finish(0, bias_land)
+    gather_relay(0, bias_sem, bias_land, (), range(chips - 1), 0)
+    gather_finish(0, bias_land, chips)
     fill(bias_f, landed(bias_land))
     mask_bias = (mask[...].astype(F32) - 1.0) * 10000.0
     extra = jnp.concatenate(
@@ -274,7 +279,6 @@
     pack = max(1, 128 // total)
     groups = width // pack
     lanes = pack * total
-    lane = lax.broadcasted_iota(jnp.int32, (groups, lanes), 1)
     two_rows, inputs = [], []
     for start in range(0, rows, pack):
         block = column[start * total : (start + pack) * total]
@@ -298,17 +302,7 @@
         inputs.append(outer_input)
 
         right_t = dot(factor_w[width:, :], outer_input, NT)
-        slabs = []
-        for place in range(pack):
-            joined = None
-            for k in range(pack):
-                piece = right_t[k * groups : (k + 1) * groups]
-                shift = ((k - place) * total) % lanes
-                if shift:
-                    piece = pltpu.roll(piece, shift, 1)
-                joined = piece if joined is None else jnp.where(lane >= k * total, piece, joined)
-            slabs.append(joined)
-        slab = jnp.concatenate(slabs, 0).astype(BF16)
+        slab = jnp.concatenate(pack_lanes(right_t, pack, total), 0).astype(BF16)
         part = (start // pack,)
         right_src[part[0]] = slab
         right_land[me, part[0]] = slab
@@ -326,66 +320,116 @@
                     (d - start) * pair_chan : (d - start + 1) * pair_chan,
                 ].astype(BF16)
 
-    for k in range(rows // pack):
-        gather_relay(2, right_sem, right_land, (k,))
-    gather_finish(2, right_land)
-    fill(right_f, landed(right_land))
-    for k in range(groups):
-        right_m[:, k * lanes : (k + 1) * lanes] = pick(right_f, k, length, groups).astype(BF16)
-
     own = pair_chan // half
-    normed = []
-    pairs = tri_left.shape[0]
-    pair_rows = rows // pairs
-    for q in range(pairs):
-        columns = pl.ds(q * pair_rows * pair_chan, pair_rows * pair_chan)
-        update = dot(right_m[...], left_t[:, columns]) * (1.0 / total)
-        sides = [[], []]
-        for k in range(pair_rows):
-            i = q * pair_rows + k
-            one = pair[i].astype(F32) + update[:, k * pair_chan : (k + 1) * pair_chan]
-            pair_one_v[i] = one
-            normed.append(layer_normalized(one).astype(BF16))
-            factors = dot(tri_t[...], normed[i], NT)
-            for side in range(2):
-                low = 2 * side * pair_chan
-                sides[side].append(
-                    jax.nn.sigmoid(factors[low + pair_chan : low + 2 * pair_chan])
-                    * factors[low : low + pair_chan]
-                )
-        tri_left[q] = by_group(sides[0], half).astype(BF16)
-        tri_right[q] = by_group(sides[1], half).astype(BF16)
-        left_land[group, q] = tri_left[q, group]
-        tri_land[me, q] = tri_right[q, group]
+    near = chips // 2 - 1
+    reach = half * rows
+    fold = max(1, 128 // reach)
+    height = pair_chan // fold
+    normed, starts = [], []
+    for turn in range(2):
+        if turn == 0:
+            steps, blocks, which = range(near), chips // 2, lax.div(me, half)
+        else:
+            steps, blocks, which = range(near, chips - 1), chips // 2, 1 - lax.div(me, half)
+        for k in range(rows // pack):
+            gather_relay(2, right_sem, right_land, (k,), steps, 2 + 4 * turn)
+        gather_finish(2 + 4 * turn, right_land, blocks)
+        fill(right_f, landed(right_land.at[pl.ds(which * half, half)]))
+        for k in range(groups):
+            right_m[:, k * lanes : (k + 1) * lanes] = pick(right_f, k, reach, groups).astype(BF16)
+        update = dot(right_m[...], left_t[...]) * (1.0 / total)
+        start = pl.multiple_of(which * reach, reach)
+        stacked = []
+        for i in range(rows):
+            one = pair[i, pl.ds(start, reach), :].astype(F32) + update[
+                :, i * pair_chan : (i + 1) * pair_chan
+            ]
+            pair_one_v[i, pl.ds(start, reach), :] = one
+            stacked.append(one)
+        normed.append(layer_normalized(jnp.concatenate(stacked, 0)).astype(BF16))
+        starts.append(start)
+        factors = dot(tri_t[...], normed[turn], NT)
+        for side, target in enumerate((tri_left, tri_right)):
+            low = 2 * side * pair_chan
+            factor = (
+                jax.nn.sigmoid(factors[low + pair_chan : low + 2 * pair_chan])
+                * factors[low : low + pair_chan]
+            )
+            wide = fold * reach
+            for base in range(rows // fold):
+                packed = pack_lanes(factor[:, base * wide : (base + 1) * wide], fold, reach)
+                for place in range(fold):
+                    at = (base * fold + place) * height
+                    fill(tri_f.at[:, pl.ds(at, height), :], packed[place])
+            for g in range(half):
+                target[turn, g] = pick(tri_f, g, rows * own // fold, half).astype(BF16)
+        left_land[which, group] = tri_left[turn, group]
+        tri_land[which, me] = tri_right[turn, group]
         spread(
-            3, lambda peer: tri_right.at[q, lax.rem(peer, half)], tri_land.at[me, q], count
+            3,
+            lambda peer: tri_right.at[turn, lax.rem(peer, half)],
+            tri_land.at[which, me],
+            count,
         )
-        spread(4, lambda peer: tri_left.at[q, lax.rem(peer, half)], left_land.at[group, q], half)
+        spread(
+            4,
+            lambda peer: tri_left.at[turn, lax.rem(peer, half)],
+            left_land.at[which, group],
+            half,
+        )
 
     ordered = dot(to_output, jnp.concatenate(two_rows, 0))
     align_out[...] = ordered.reshape(total, rows, channels).astype(BF16)
-    for i in range(rows):
-        gate_v[i] = jax.nn.sigmoid(dot(normed[i], tri_w[:, 4 * pair_chan :]))
-    taken(tri_land.at[pl.ds(0, count - 1)], recv_sem.at[3])
-    taken(left_land.at[pl.ds(0, half - 1)], recv_sem.at[4])
+    for turn in range(2):
+        opened = jax.nn.sigmoid(dot(normed[turn], tri_w[:, 4 * pair_chan :]))
+        for i in range(rows):
+            gate_v[i, pl.ds(starts[turn], reach), :] = opened[i * reach : (i + 1) * reach]
+
+    taken(tri_land.at[pl.ds(0, 2), pl.ds(0, count - 1)], recv_sem.at[3])
+    taken(left_land.at[pl.ds(0, 2), pl.ds(0, half - 1)], recv_sem.at[4])
     fill(land_f, landed(tri_land))
     fill(left_f, landed(left_land))
+    slab_rows = rows * own // fold
     block = half * rows
-    for c in range(own):
+    lane = lax.broadcasted_iota(jnp.int32, (1, fold * reach), 1)
+    folds = [
+        jnp.where((lane >= k * reach) & (lane < (k + 1) * reach), 1.0, 0.0).astype(BF16)
+        for k in range(fold)
+    ]
+    for c in range(own // fold):
+        step = own // fold
+        left_sides = [
+            jnp.concatenate(
+                [
+                    pick(left_f, q * half * slab_rows + i * step + c, half, slab_rows)
+                    for i in range(rows)
+                ],
+                0,
+            ).astype(BF16)
+            for q in range(2)
+        ]
+        right_side = jnp.concatenate(
+            [pick(land_f, q * count * slab_rows + c, length, step) for q in range(2)], 1
+        ).astype(BF16)
         left_side = jnp.concatenate(
-            [pick(left_f, i * own + c, half, own * rows) for i in range(rows)], 0
-        ).astype(BF16)
-        right_side = pick(land_f, c, length, own).astype(BF16)
-        fill(comb_f.at[:, pl.ds(c * block, block), :], dot(left_side, right_side, NT))
+            [jnp.concatenate([side * m for side in left_sides], 1) for m in folds], 0
+        )
+        product = dot(left_side, right_side, NT)
+        for k in range(fold):
+            fill(
+                comb_f.at[:, pl.ds((k * step + c) * block, block), :],
+                product[k * block : (k + 1) * block],
+            )
     for p in range(half):
         back_src[p] = pick(comb_f, p, own * rows, half).astype(BF16)
     back_land[group] = back_src[group]
     spread(5, lambda peer: back_src.at[lax.rem(peer, half)], back_land.at[group], half)
 
     taken(back_land.at[pl.ds(0, half - 1)], recv_sem.at[5])
-    for number, sent in enumerate((bias_land, msa_land, right_land, tri_land)):
+    for number, sent in enumerate((bias_land, msa_land, right_land)):
         taken(sent.at[pl.ds(0, count - 1)], send_sem.at[number])
-    taken(left_land.at[pl.ds(0, half - 1)], send_sem.at[4])
+    taken(tri_land.at[pl.ds(0, 2), pl.ds(0, count - 1)], send_sem.at[3])
+    taken(left_land.at[pl.ds(0, 2), pl.ds(0, half - 1)], send_sem.at[4])
     taken(back_land.at[pl.ds(0, half - 1)], send_sem.at[5])
 
 
@@ -393,8 +437,11 @@
     store_align = pltpu.make_async_copy(align, align_out, sem.at[0])
     store_align.start()
     fill(back_f, landed(back_land))
+    owners = back_land.shape[0]
+    own = back_land.shape[1] // rows
     for i in range(rows):
-        combined = layer_normalized(pick(back_f, i, pair_one.shape[2], rows), 0).astype(BF16)
+        channels = [pick(back_f, c * rows + i, owners, own * rows) for c in range(own)]
+        combined = layer_normalized(jnp.concatenate(channels, 0), 0).astype(BF16)
         result = pair_one[i] + gate[i] * dot(combined, tri_o[...], TN)
         pair_v[i] = result.astype(BF16)
     store_pair = pltpu.make_async_copy(pair_v, pair_out, sem.at[1])
@@ -446,8 +493,10 @@
     ]
     lane_parts = channels // 128
     vmem = pltpu.VMEM
-    parts, pairs = rows // pack, 2
-    tri_slab = (pairs, half, own * rows // pairs, length)
+    parts = rows // pack
+    reach = half * rows
+    fold = max(1, 128 // reach)
+    tri_slab = (rows * own // fold, fold * reach)
     exchanges = [
         vmem((heads * rows, length), BF16),
         vmem((count, heads * rows, length), BF16),
@@ -455,10 +504,10 @@
         vmem((count, lane_parts * seqs * rows, 128), BF16),
         vmem((parts, groups * pack, lanes), BF16),
         vmem((count, parts, groups * pack, lanes), BF16),
-        vmem(tri_slab, BF16),
-        vmem((half, pairs) + tri_slab[2:], BF16),
-        vmem(tri_slab, BF16),
-        vmem((count, pairs) + tri_slab[2:], BF16),
+        vmem((2, half) + tri_slab, BF16),
+        vmem((2, half) + tri_slab, BF16),
+        vmem((2, half) + tri_slab, BF16),
+        vmem((2, count) + tri_slab, BF16),
         vmem((half, own * rows, length), BF16),
     ]
 
@@ -474,15 +523,16 @@
             pieces(width * width, pair_chan),
             vmem((width, width * pair_chan), BF16),
             vmem((width * total, rows * pair_chan), BF16),
-            pieces(length * groups, lanes),
-            vmem((length, width * total), BF16),
+            pieces(reach * groups, lanes),
+            vmem((reach, width * total), BF16),
             vmem((4 * pair_chan, pair_chan), BF16),
-            pieces(count * own * rows, length),
-            pieces(half * own * rows, length),
+            pieces(rows * pair_chan // fold, fold * reach),
+            pieces(2 * count * tri_slab[0], tri_slab[1]),
+            pieces(2 * half * tri_slab[0], tri_slab[1]),
             pieces(half * own * rows, length),
             pltpu.SemaphoreType.DMA((len(operands),)),
             pltpu.SemaphoreType.DMA((6,)),
-            pltpu.SemaphoreType.DMA((6,)),
+            pltpu.SemaphoreType.DMA((7,)),
             pltpu.SemaphoreType.DMA((half - 1,)),
             pltpu.SemaphoreType.DMA((parts, half - 1)),
         ]

time: 46.7 us -> 44.6 us (0.955)
  Pallas kernels: 45.9 us -> 43.8 us
    pallas_call x1, Pallas kernels: 44.9 us -> 42.7 us  [shards(): pl.pallas_call(functools.partial(block_kernel, sizes), out_shape=(jax.Sha...]
where the time goes in v4:
time: 44.6 us; the launch traced here: 44.5 us
  Pallas kernels  43.8 us (98%)
  between operations  0.66 us (1%)
    pallas_call x1, Pallas kernels, shards(): pl.pallas_call(functools.partial(block_kernel, sizes), out_shape=(jax.Sha...  42.7 us
    pallas_call x1, Pallas kernels, shards(): pl.pallas_call(functools.partial(finish_kernel, rows), out_shape=(jax.Sha...  1.08 us

profile of v4, /device:TPU:0, one launch (start us, length us, event | category | flops | bytes accessed | tf_op | source)
XLA Modules:
  0.0 44.5 jit_solution(14503104723635371212)
XLA Ops:
  0.6 0.0 copy-start
  0.6 42.7 %shard_map.149 = (bf16[64,4,256]{2,1,0:T(4,128)(2,1)S(1)}, bf16[16,32,128]{2,1,0:T(8,128)(2,1)S(1)}, f32[4,128,128]{2,1,0:T(8,128)S(1)}, f32[4,128,128]{2,1,0:T(8,128)S(1)}) custom-call(s32[2,128]{1,0:T(2,128)} %ids_h.1, s32[1,128]{1,0:T(1,128)} %bitcast.5, bf16[2,128,256]{2,1,0:T(8,128)(2,1)} %align_h.1, bf16[4,128,128]{2,1,0:T(8,128)(2,1)} %pair_h.1, ...), custom_call_target="tpu_custom_call" | custom-call | tf_op jit(solution)/shard_map/pallas_call | solution.py:543
  43.4 0.0 copy-done
  43.4 1.1 %shard_map.150 = (bf16[64,4,256]{2,1,0:T(4,128)(2,1)}, bf16[4,128,128]{2,1,0:T(8,128)(2,1)}) custom-call(bf16[64,4,256]{2,1,0:T(4,128)(2,1)S(1)} %get-tuple-element.6.align, bf16[16,32,128]{2,1,0:T(8,128)(2,1)S(1)} %get-tuple-element.7.back_land, f32[4,128,128]{2,1,0:T(8,128)S(1)} %get-tuple-element.8.pair_one, f32[4,128,128]{2,1,0:T(8,128)S(1)} %get-tuple-element.9.gate, ...), custom_call_target="tpu_custom_call" | custom-call | tf_op jit(solution)/shard_map/pallas_call | solution.py:558
Async XLA Ops:
  0.6 42.8 %copy-start = (bf16[128,128]{1,0:T(8,128)(2,1)S(1)}, bf16[128,128]{1,0:T(8,128)(2,1)}, u32[]{:S(2)}) copy-start(bf16[128,128]{1,0:T(8,128)(2,1)} %tri_o.1) | copy-start | bytes 98308

commit v5 on v4

--- a/solution.py
+++ b/solution.py
@@ -81,10 +81,27 @@
     return packed
 
 
-def softmax_rows(scores):
-    top = jnp.max(scores, -1, keepdims=True)
-    powers = jnp.exp(scores - top)
-    return (powers / jnp.sum(powers, -1, keepdims=True)).astype(BF16)
+def attend(scores, values, ones):
+    powers = jnp.exp(scores - jnp.max(scores, -1, keepdims=True)).astype(BF16)
+    side = jnp.concatenate([powers[h] for h in range(powers.shape[0])], 1)
+    return dot(side, values) / dot(side, ones)
+
+
+def interleave(blocks, rows):
+    owners, lanes = blocks[0].shape[0] // rows, blocks[0].shape[1]
+    if len(blocks) == 2 and rows == 4:
+        one, two = [b.reshape(owners // 2, 8, lanes) for b in blocks]
+        low = lax.broadcasted_iota(jnp.int32, one.shape, 1) < rows
+        even = jnp.where(low, one, pltpu.roll(two, rows, 1))
+        odd = jnp.where(low, pltpu.roll(one, rows, 1), two)
+        return jnp.stack([even, odd], 1).reshape(owners, 8, lanes)
+    return jnp.stack(
+        [
+            jnp.concatenate([b[p * rows : (p + 1) * rows] for b in blocks], 0)
+            for p in range(owners)
+        ],
+        0,
+    )
 
 
 def block_kernel(
@@ -97,7 +114,7 @@
     bias_src, bias_land, msa_src, msa_land, right_src, right_land, tri_left, left_land,
     tri_right, tri_land, back_src,
     bias_f, msa_f, outer_f, outer_w2, left_t, right_f, right_m, tri_t,
-    tri_f, land_f, left_f, comb_f,
+    tri_f, land_f, left_f, comb_f, zero_v, raw_v, value_v, open_v,
     in_sem, send_sem, recv_sem, bias_sem, right_sem,
 ):
     count, seqs, rows, length, channels, heads, width, pair_chan, total = sizes
@@ -162,13 +179,12 @@
     half = count // 2
     group, first = lax.rem(me, half), lax.div(me, half) * half
 
-    def spread(number, source, landing, size):
-        @pl.loop(1, size)
+    def spread(number, source, landing, size, base=0, skip=1):
+        place = me if size == count else group
+
+        @pl.loop(skip, size)
         def _(step):
-            if size == count:
-                peer = lax.rem(me + step, count)
-            else:
-                peer = first + lax.rem(group + step, size)
+            peer = base + lax.rem(place + step, size)
             remote(source(peer), landing, number, recv_sem.at[number], peer)
 
     loads[0].wait()
@@ -197,23 +213,19 @@
 
     loads[6].wait()
     loads[7].wait()
-    raw_scores, spread_values = [], []
-    for s in range(seqs):
-        part = projected[s * length : (s + 1) * length]
+    def by_head(block):
+        return jnp.concatenate([block * m for m in masks], 0)
+
+    def split(part):
         query = (part[:, :channels] * scale).astype(BF16)
         key = part[:, channels : 2 * channels].astype(BF16)
         value = part[:, 2 * channels : 3 * channels].astype(BF16)
-        stacked = jnp.concatenate([query * m for m in masks], 0)
-        raw_scores.append(dot(stacked, key, NT))
-        spread_values.append(jnp.concatenate([value * m for m in masks], 0))
-    to_owner = selection(
-        seqs * length,
-        lambda o: (
-            split_index(split_index(o, rows)[0], seqs)[1] * length
-            + split_index(o, seqs * rows)[0] * rows
-            + split_index(o, rows)[1]
-        ),
-    )
+        scores = dot(by_head(query), key, NT).reshape(heads, query.shape[0], key.shape[0])
+        return scores, by_head(value), jax.nn.sigmoid(part[:, 3 * channels :])
+
+    zero_v[...] = msa_zero.reshape(zero_v.shape)
+    for s in range(seqs):
+        raw_v[s], value_v[s], open_v[s] = split(projected[s * length : (s + 1) * length])
     for load in loads[8:]:
         load.wait()
     tri_t[...] = jnp.transpose(tri_w[:, : 4 * pair_chan].astype(F32), (1, 0)).astype(BF16)
@@ -223,33 +235,43 @@
             outer_f, d, width, width
         ).astype(BF16)
 
-    gather_relay(0, bias_sem, bias_land, (), range(chips - 1), 0)
-    gather_finish(0, bias_land, chips)
-    fill(bias_f, landed(bias_land))
+    near, reach = chips // 2 - 1, half * rows
+    mine = lax.div(me, half)
+    turns = (
+        (range(near), mine, pl.multiple_of(mine * reach, reach)),
+        (range(near, chips - 1), 1 - mine, pl.multiple_of((1 - mine) * reach, reach)),
+    )
     mask_bias = (mask[...].astype(F32) - 1.0) * 10000.0
-    extra = jnp.concatenate(
-        [pick(bias_f, h, length, heads) for h in range(heads)], 0
-    ) + mask_bias
-    one_rows = []
-    for s in range(seqs):
-        weights = softmax_rows(raw_scores[s] + extra)
-        side = jnp.concatenate(
-            [weights[h * length : (h + 1) * length] for h in range(heads)], 1
+    row_ones = by_head(jnp.ones((length, channels), BF16))
+    lane_parts = channels // 128
+    for turn, (steps, which, start) in enumerate(turns):
+        gather_relay(0, bias_sem, bias_land, (), steps, 7 * turn)
+        gather_finish(7 * turn, bias_land, chips // 2)
+        fill(bias_f, landed(bias_land.at[pl.ds(which * half, half)]))
+        extra = jnp.stack([pick(bias_f, h, reach, heads) for h in range(heads)], 0) + mask_bias
+        gated = []
+        for s in range(seqs):
+            mixed = attend(raw_v[s, :, pl.ds(start, reach), :] + extra, value_v[s], row_ones)
+            gated.append((open_v[s, pl.ds(start, reach), :] * mixed).astype(BF16))
+        added = dot(jnp.concatenate(gated, 0), row_o[...])
+        blocks = [
+            zero_v[s, pl.ds(start, reach), :] + added[s * reach : (s + 1) * reach]
+            for s in range(seqs)
+        ]
+        ordered = interleave(blocks, rows)
+        msa_src[pl.ds(which * half, half)] = jnp.concatenate(
+            [ordered[:, :, k * 128 : (k + 1) * 128] for k in range(lane_parts)], 1
+        ).astype(BF16)
+        if turn == 0:
+            msa_land[me] = msa_src[me]
+        spread(
+            1,
+            lambda peer: msa_src.at[peer],
+            msa_land.at[me],
+            half,
+            first if turn == 0 else half - first,
+            1 - turn,
         )
-        mixed = dot(side, spread_values[s])
-        gate = projected[s * length : (s + 1) * length, 3 * channels :]
-        gated = (jax.nn.sigmoid(gate) * mixed).astype(BF16)
-        zero = msa_zero[s * length : (s + 1) * length]
-        one_rows.append((zero + dot(gated, row_o[...])).astype(BF16))
-    ordered = dot(to_owner, jnp.concatenate(one_rows, 0))
-    ordered = ordered.reshape(count, seqs * rows, channels)
-    lane_parts = channels // 128
-    slabs = jnp.concatenate(
-        [ordered[:, :, k * 128 : (k + 1) * 128] for k in range(lane_parts)], 1
-    ).astype(BF16)
-    msa_src[...] = slabs
-    msa_land[me] = msa_src[me]
-    spread(1, lambda peer: msa_src.at[peer], msa_land.at[me], count)
 
     to_output = selection(
         total * rows,
@@ -279,24 +301,20 @@
     pack = max(1, 128 // total)
     groups = width // pack
     lanes = pack * total
+    column_ones = by_head(jnp.ones((lanes, channels), BF16))
+    together = (
+        split_index(lax.broadcasted_iota(jnp.int32, (1, lanes, lanes), 1), total)[0]
+        == split_index(lax.broadcasted_iota(jnp.int32, (1, lanes, lanes), 2), total)[0]
+    )
     two_rows, inputs = [], []
     for start in range(0, rows, pack):
         block = column[start * total : (start + pack) * total]
         projected = dot(layer_normalized(block).astype(BF16), col_w[...])
-        gated_rows = []
-        for i in range(pack):
-            part = projected[i * total : (i + 1) * total]
-            query = (part[:, :channels] * scale).astype(BF16)
-            key = part[:, channels : 2 * channels].astype(BF16)
-            value = part[:, 2 * channels : 3 * channels].astype(BF16)
-            stacked = jnp.concatenate([query * m for m in masks], 0)
-            weights = softmax_rows(dot(stacked, key, NT))
-            every = dot(weights, value)
-            mixed = every[:total] * masks[0].astype(F32)
-            for h in range(1, heads):
-                mixed = mixed + every[h * total : (h + 1) * total] * masks[h].astype(F32)
-            gated_rows.append((jax.nn.sigmoid(part[:, 3 * channels :]) * mixed).astype(BF16))
-        msa_two = block + dot(jnp.concatenate(gated_rows, 0), col_o[...])
+        scores, value, opened = split(projected)
+        if pack > 1:
+            scores = jnp.where(together, scores, -1e30)
+        gated = (opened * attend(scores, value, column_ones)).astype(BF16)
+        msa_two = block + dot(gated, col_o[...])
         outer_input = layer_normalized(msa_two).astype(BF16)
         two_rows.append(msa_two.astype(BF16))
         inputs.append(outer_input)
@@ -321,24 +339,17 @@
                 ].astype(BF16)
 
     own = pair_chan // half
-    near = chips // 2 - 1
-    reach = half * rows
     fold = max(1, 128 // reach)
     height = pair_chan // fold
-    normed, starts = [], []
-    for turn in range(2):
-        if turn == 0:
-            steps, blocks, which = range(near), chips // 2, lax.div(me, half)
-        else:
-            steps, blocks, which = range(near, chips - 1), chips // 2, 1 - lax.div(me, half)
+    normed = []
+    for turn, (steps, which, start) in enumerate(turns):
         for k in range(rows // pack):
             gather_relay(2, right_sem, right_land, (k,), steps, 2 + 4 * turn)
-        gather_finish(2 + 4 * turn, right_land, blocks)
+        gather_finish(2 + 4 * turn, right_land, chips // 2)
         fill(right_f, landed(right_land.at[pl.ds(which * half, half)]))
         for k in range(groups):
             right_m[:, k * lanes : (k + 1) * lanes] = pick(right_f, k, reach, groups).astype(BF16)
         update = dot(right_m[...], left_t[...]) * (1.0 / total)
-        start = pl.multiple_of(which * reach, reach)
         stacked = []
         for i in range(rows):
             one = pair[i, pl.ds(start, reach), :].astype(F32) + update[
@@ -347,7 +358,6 @@
             pair_one_v[i, pl.ds(start, reach), :] = one
             stacked.append(one)
         normed.append(layer_normalized(jnp.concatenate(stacked, 0)).astype(BF16))
-        starts.append(start)
         factors = dot(tri_t[...], normed[turn], NT)
         for side, target in enumerate((tri_left, tri_right)):
             low = 2 * side * pair_chan
@@ -376,6 +386,7 @@
             lambda peer: tri_left.at[turn, lax.rem(peer, half)],
             left_land.at[which, group],
             half,
+            first,
         )
 
     ordered = dot(to_output, jnp.concatenate(two_rows, 0))
@@ -383,7 +394,7 @@
     for turn in range(2):
         opened = jax.nn.sigmoid(dot(normed[turn], tri_w[:, 4 * pair_chan :]))
         for i in range(rows):
-            gate_v[i, pl.ds(starts[turn], reach), :] = opened[i * reach : (i + 1) * reach]
+            gate_v[i, pl.ds(turns[turn][2], reach), :] = opened[i * reach : (i + 1) * reach]
 
     taken(tri_land.at[pl.ds(0, 2), pl.ds(0, count - 1)], recv_sem.at[3])
     taken(left_land.at[pl.ds(0, 2), pl.ds(0, half - 1)], recv_sem.at[4])
@@ -423,7 +434,7 @@
     for p in range(half):
         back_src[p] = pick(comb_f, p, own * rows, half).astype(BF16)
     back_land[group] = back_src[group]
-    spread(5, lambda peer: back_src.at[lax.rem(peer, half)], back_land.at[group], half)
+    spread(5, lambda peer: back_src.at[lax.rem(peer, half)], back_land.at[group], half, first)
 
     taken(back_land.at[pl.ds(0, half - 1)], recv_sem.at[5])
     for number, sent in enumerate((bias_land, msa_land, right_land)):
@@ -518,7 +529,7 @@
         [vmem(x.shape, x.dtype) for x in operands]
         + exchanges
         + [
-            pieces(count * heads * rows, length),
+            pieces(half * heads * rows, length),
             pieces(count * lane_parts * seqs * rows, 128),
             pieces(width * width, pair_chan),
             vmem((width, width * pair_chan), BF16),
@@ -530,9 +541,13 @@
             pieces(2 * count * tri_slab[0], tri_slab[1]),
             pieces(2 * half * tri_slab[0], tri_slab[1]),
             pieces(half * own * rows, length),
+            vmem((seqs, length, channels), F32),
+            vmem((seqs, heads, length, length), F32),
+            vmem((seqs, heads * length, channels), BF16),
+            vmem((seqs, length, channels), F32),
             pltpu.SemaphoreType.DMA((len(operands),)),
             pltpu.SemaphoreType.DMA((6,)),
-            pltpu.SemaphoreType.DMA((7,)),
+            pltpu.SemaphoreType.DMA((8,)),
             pltpu.SemaphoreType.DMA((half - 1,)),
             pltpu.SemaphoreType.DMA((parts, half - 1)),
         ]

time: 44.6 us -> 43.9 us (0.984)
  Pallas kernels: 43.8 us -> 43 us
    pallas_call x1, Pallas kernels: 42.7 us -> 42 us  [shards(): pl.pallas_call(functools.partial(block_kernel, sizes), out_shape=(jax.Sha...]
where the time goes in v5:
time: 43.9 us; the launch traced here: 43.7 us
  Pallas kernels  43 us (98%)
  between operations  0.66 us (2%)
    pallas_call x1, Pallas kernels, shards(): pl.pallas_call(functools.partial(block_kernel, sizes), out_shape=(jax.Sha...  42 us
    pallas_call x1, Pallas kernels, shards(): pl.pallas_call(functools.partial(finish_kernel, rows), out_shape=(jax.Sha...  1.08 us

profile of v5, /device:TPU:0, one launch (start us, length us, event | category | flops | bytes accessed | tf_op | source)
XLA Modules:
  0.0 43.7 jit_solution(17649320227321896916)
XLA Ops:
  0.6 0.0 copy-start
  0.6 42.0 %shard_map.149 = (bf16[64,4,256]{2,1,0:T(4,128)(2,1)S(1)}, bf16[16,32,128]{2,1,0:T(8,128)(2,1)S(1)}, f32[4,128,128]{2,1,0:T(8,128)S(1)}, f32[4,128,128]{2,1,0:T(8,128)S(1)}) custom-call(s32[2,128]{1,0:T(2,128)} %ids_h.1, s32[1,128]{1,0:T(1,128)} %bitcast.5, bf16[2,128,256]{2,1,0:T(8,128)(2,1)} %align_h.1, bf16[4,128,128]{2,1,0:T(8,128)(2,1)} %pair_h.1, ...), custom_call_target="tpu_custom_call" | custom-call | tf_op jit(solution)/shard_map/pallas_call | solution.py:558
  42.6 0.0 copy-done
  42.6 1.1 %shard_map.150 = (bf16[64,4,256]{2,1,0:T(4,128)(2,1)}, bf16[4,128,128]{2,1,0:T(8,128)(2,1)}) custom-call(bf16[64,4,256]{2,1,0:T(4,128)(2,1)S(1)} %get-tuple-element.6.align, bf16[16,32,128]{2,1,0:T(8,128)(2,1)S(1)} %get-tuple-element.7.back_land, f32[4,128,128]{2,1,0:T(8,128)S(1)} %get-tuple-element.8.pair_one, f32[4,128,128]{2,1,0:T(8,128)S(1)} %get-tuple-element.9.gate, ...), custom_call_target="tpu_custom_call" | custom-call | tf_op jit(solution)/shard_map/pallas_call | solution.py:573
Async XLA Ops:
  0.6 42.0 %copy-start = (bf16[128,128]{1,0:T(8,128)(2,1)S(1)}, bf16[128,128]{1,0:T(8,128)(2,1)}, u32[]{:S(2)}) copy-start(bf16[128,128]{1,0:T(8,128)(2,1)} %tri_o.1) | copy-start | bytes 98308

commit v6 on v5

--- a/solution.py
+++ b/solution.py
@@ -122,8 +122,7 @@
     me = lax.axis_index("res")
     barrier = pltpu.get_barrier_semaphore()
 
-    @pl.loop(1, count)
-    def _(step):
+    for step in range(1, count):
         pl.semaphore_signal(
             barrier, inc=1, device_id={"res": lax.rem(me + step, count)}, device_id_type=MESH
         )
@@ -156,16 +155,28 @@
     chips = count // 2
     partner = me + 1 - 2 * lax.rem(me, 2)
     flips = [
-        (1 - 2 * lax.rem(lax.div(me, 2 << j), 2)) * (2 << j) for j in range(chips.bit_length() - 1)
+        (1 - 2 * lax.rem(lax.div(me, 1 << j), 2)) * (1 << j) for j in range(count.bit_length() - 1)
     ]
-    others = [me + sum(flips[j] for j in range(len(flips)) if (k >> j) & 1) for k in range(1, chips)]
-
-    def gather_start(number, arrivals, source, landing, part):
-        for k in reversed(range(chips - 1)):
+
+    def across(k):
+        return me + sum(flips[j] for j in range(len(flips)) if (k >> j) & 1)
+
+    others = [across(2 * k) for k in range(1, chips)]
+
+    def gather_start(number, arrivals, source, landing, part, reached=None):
+        for k in reversed(range(chips - 1 if reached is None else reached)):
             remote(
                 source, landing.at[(me,) + part], number, arrivals.at[part + (k,)], others[k]
             )
         remote(source, landing.at[(me,) + part], number, recv_sem.at[number], partner)
+
+    def gather_forward(number, arrivals, landing, part):
+        last = chips // 2 - 1
+        block = landing.at[(others[last],) + part]
+        taken(block, arrivals.at[part + (last,)])
+        for k in reversed(range(last)):
+            remote(block, block, number, arrivals.at[part + (k + chips // 2,)], others[k])
+        remote(block, block, number, recv_sem.at[6], partner)
 
     def gather_relay(number, arrivals, landing, part, steps, handed):
         for k in steps:
@@ -177,15 +188,14 @@
         taken(landing.at[pl.ds(0, blocks)], recv_sem.at[handed])
 
     half = count // 2
-    group, first = lax.rem(me, half), lax.div(me, half) * half
-
-    def spread(number, source, landing, size, base=0, skip=1):
-        place = me if size == count else group
-
-        @pl.loop(skip, size)
-        def _(step):
-            peer = base + lax.rem(place + step, size)
+    group = lax.rem(me, half)
+
+    def spread(number, source, landing, distances):
+        for k in reversed(distances):
+            peer = across(k)
             remote(source(peer), landing, number, recv_sem.at[number], peer)
+
+    everyone, own_half, other_half = range(1, count), range(1, half), range(half, count)
 
     loads[0].wait()
     loads[1].wait()
@@ -268,9 +278,7 @@
             1,
             lambda peer: msa_src.at[peer],
             msa_land.at[me],
-            half,
-            first if turn == 0 else half - first,
-            1 - turn,
+            own_half if turn == 0 else other_half,
         )
 
     to_output = selection(
@@ -324,7 +332,11 @@
         part = (start // pack,)
         right_src[part[0]] = slab
         right_land[me, part[0]] = slab
-        gather_start(2, right_sem, right_src.at[part[0]], right_land, part)
+        forwarded = part[0] < rows // pack // 2
+        gather_start(
+            2, right_sem, right_src.at[part[0]], right_land, part,
+            chips // 2 if forwarded else None,
+        )
 
     left = dot(jnp.concatenate(inputs, 0), factor_w[:width, :], NT).astype(BF16)
     chunk = 8
@@ -344,7 +356,11 @@
     normed = []
     for turn, (steps, which, start) in enumerate(turns):
         for k in range(rows // pack):
-            gather_relay(2, right_sem, right_land, (k,), steps, 2 + 4 * turn)
+            mirrored = k < rows // pack // 2
+            if turn == 0 and mirrored:
+                gather_forward(2, right_sem, right_land, (k,))
+            left_over = [x for x in steps if not (turn == 1 and mirrored and x == near)]
+            gather_relay(2, right_sem, right_land, (k,), left_over, 2 + 4 * turn)
         gather_finish(2 + 4 * turn, right_land, chips // 2)
         fill(right_f, landed(right_land.at[pl.ds(which * half, half)]))
         for k in range(groups):
@@ -379,14 +395,13 @@
             3,
             lambda peer: tri_right.at[turn, lax.rem(peer, half)],
             tri_land.at[which, me],
-            count,
+            everyone,
         )
         spread(
             4,
             lambda peer: tri_left.at[turn, lax.rem(peer, half)],
             left_land.at[which, group],
-            half,
-            first,
+            own_half,
         )
 
     ordered = dot(to_output, jnp.concatenate(two_rows, 0))
@@ -434,7 +449,7 @@
     for p in range(half):
         back_src[p] = pick(comb_f, p, own * rows, half).astype(BF16)
     back_land[group] = back_src[group]
-    spread(5, lambda peer: back_src.at[lax.rem(peer, half)], back_land.at[group], half, first)
+    spread(5, lambda peer: back_src.at[lax.rem(peer, half)], back_land.at[group], own_half)
 
     taken(back_land.at[pl.ds(0, half - 1)], recv_sem.at[5])
     for number, sent in enumerate((bias_land, msa_land, right_land)):

time: 43.9 us -> 42.8 us (0.975)
  Pallas kernels: 43 us -> 42 us
    pallas_call x1, Pallas kernels: 42 us -> 40.9 us  [shards(): pl.pallas_call(functools.partial(block_kernel, sizes), out_shape=(jax.Sha...]
where the time goes in v6:
time: 42.8 us; the launch traced here: 42.6 us
  Pallas kernels  42 us (98%)
  between operations  0.66 us (2%)
    pallas_call x1, Pallas kernels, shards(): pl.pallas_call(functools.partial(block_kernel, sizes), out_shape=(jax.Sha...  40.9 us
    pallas_call x1, Pallas kernels, shards(): pl.pallas_call(functools.partial(finish_kernel, rows), out_shape=(jax.Sha...  1.08 us

profile of v6, /device:TPU:0, one launch (start us, length us, event | category | flops | bytes accessed | tf_op | source)
XLA Modules:
  0.0 42.6 jit_solution(12937284746330270430)
XLA Ops:
  0.6 0.0 copy-start
  0.6 40.9 %shard_map.149 = (bf16[64,4,256]{2,1,0:T(4,128)(2,1)S(1)}, bf16[16,32,128]{2,1,0:T(8,128)(2,1)S(1)}, f32[4,128,128]{2,1,0:T(8,128)S(1)}, f32[4,128,128]{2,1,0:T(8,128)S(1)}) custom-call(s32[2,128]{1,0:T(2,128)} %ids_h.1, s32[1,128]{1,0:T(1,128)} %bitcast.5, bf16[2,128,256]{2,1,0:T(8,128)(2,1)} %align_h.1, bf16[4,128,128]{2,1,0:T(8,128)(2,1)} %pair_h.1, ...), custom_call_target="tpu_custom_call" | custom-call | tf_op jit(solution)/shard_map/pallas_call | solution.py:573
  41.5 0.0 copy-done
  41.6 1.1 %shard_map.150 = (bf16[64,4,256]{2,1,0:T(4,128)(2,1)}, bf16[4,128,128]{2,1,0:T(8,128)(2,1)}) custom-call(bf16[64,4,256]{2,1,0:T(4,128)(2,1)S(1)} %get-tuple-element.6.align, bf16[16,32,128]{2,1,0:T(8,128)(2,1)S(1)} %get-tuple-element.7.back_land, f32[4,128,128]{2,1,0:T(8,128)S(1)} %get-tuple-element.8.pair_one, f32[4,128,128]{2,1,0:T(8,128)S(1)} %get-tuple-element.9.gate, ...), custom_call_target="tpu_custom_call" | custom-call | tf_op jit(solution)/shard_map/pallas_call | solution.py:588
Async XLA Ops:
  0.6 40.9 %copy-start = (bf16[128,128]{1,0:T(8,128)(2,1)S(1)}, bf16[128,128]{1,0:T(8,128)(2,1)}, u32[]{:S(2)}) copy-start(bf16[128,128]{1,0:T(8,128)(2,1)} %tri_o.1) | copy-start | bytes 98308

commit v7 on v6

--- a/solution.py
+++ b/solution.py
@@ -120,12 +120,18 @@
     count, seqs, rows, length, channels, heads, width, pair_chan, total = sizes
     head_size = channels // heads
     me = lax.axis_index("res")
+    half = count // 2
+    flips = [
+        (1 - 2 * lax.rem(lax.div(me, 1 << j), 2)) * (1 << j) for j in range(count.bit_length() - 1)
+    ]
+
+    def across(k):
+        return me + sum(flips[j] for j in range(len(flips)) if (k >> j) & 1)
+
+    mirror = across(half)
     barrier = pltpu.get_barrier_semaphore()
-
-    for step in range(1, count):
-        pl.semaphore_signal(
-            barrier, inc=1, device_id={"res": lax.rem(me + step, count)}, device_id_type=MESH
-        )
+    for k in reversed(range(1, half + 1)):
+        pl.semaphore_signal(barrier, inc=1, device_id={"res": across(k)}, device_id_type=MESH)
 
     staged = [
         (pair_h, pair), (bias_w_h, bias_w), (align_h, align), (ids_h, ids), (table_h, table),
@@ -152,42 +158,17 @@
     def taken(landing, semaphore):
         pltpu.make_async_copy(landing, landing, semaphore).wait()
 
-    chips = count // 2
-    partner = me + 1 - 2 * lax.rem(me, 2)
-    flips = [
-        (1 - 2 * lax.rem(lax.div(me, 1 << j), 2)) * (1 << j) for j in range(count.bit_length() - 1)
-    ]
-
-    def across(k):
-        return me + sum(flips[j] for j in range(len(flips)) if (k >> j) & 1)
-
-    others = [across(2 * k) for k in range(1, chips)]
-
-    def gather_start(number, arrivals, source, landing, part, reached=None):
-        for k in reversed(range(chips - 1 if reached is None else reached)):
-            remote(
-                source, landing.at[(me,) + part], number, arrivals.at[part + (k,)], others[k]
-            )
-        remote(source, landing.at[(me,) + part], number, recv_sem.at[number], partner)
-
-    def gather_forward(number, arrivals, landing, part):
-        last = chips // 2 - 1
-        block = landing.at[(others[last],) + part]
-        taken(block, arrivals.at[part + (last,)])
-        for k in reversed(range(last)):
-            remote(block, block, number, arrivals.at[part + (k + chips // 2,)], others[k])
-        remote(block, block, number, recv_sem.at[6], partner)
-
-    def gather_relay(number, arrivals, landing, part, steps, handed):
-        for k in steps:
-            block = landing.at[(others[k],) + part]
-            taken(block, arrivals.at[part + (k,)])
-            remote(block, block, number, recv_sem.at[handed], partner)
-
-    def gather_finish(handed, landing, blocks):
-        taken(landing.at[pl.ds(0, blocks)], recv_sem.at[handed])
-
-    half = count // 2
+    def gather_start(number, mirrored, source, landing, part=()):
+        remote(source, landing.at[(me,) + part], number, mirrored, mirror)
+        for k in reversed(range(1, half)):
+            remote(source, landing.at[(me,) + part], number, recv_sem.at[number], across(k))
+
+    def gather_forward(number, mirrored, landing, handed, part=()):
+        block = landing.at[(mirror,) + part]
+        taken(block, mirrored)
+        for k in reversed(range(1, half)):
+            remote(block, block, number, recv_sem.at[handed], across(k))
+
     group = lax.rem(me, half)
 
     def spread(number, source, landing, distances):
@@ -206,8 +187,6 @@
     slab = jnp.concatenate(pieces, 0).astype(BF16)
     bias_src[...] = slab
     bias_land[me] = slab
-    pl.semaphore_wait(barrier, count - 1)
-    gather_start(0, bias_sem, bias_src, bias_land, ())
 
     for load in loads[2:6]:
         load.wait()
@@ -236,6 +215,9 @@
     zero_v[...] = msa_zero.reshape(zero_v.shape)
     for s in range(seqs):
         raw_v[s], value_v[s], open_v[s] = split(projected[s * length : (s + 1) * length])
+    pl.semaphore_wait(barrier, half)
+    gather_start(0, bias_sem.at[0], bias_src, bias_land)
+
     for load in loads[8:]:
         load.wait()
     tri_t[...] = jnp.transpose(tri_w[:, : 4 * pair_chan].astype(F32), (1, 0)).astype(BF16)
@@ -245,18 +227,19 @@
             outer_f, d, width, width
         ).astype(BF16)
 
-    near, reach = chips // 2 - 1, half * rows
+    reach = half * rows
     mine = lax.div(me, half)
     turns = (
-        (range(near), mine, pl.multiple_of(mine * reach, reach)),
-        (range(near, chips - 1), 1 - mine, pl.multiple_of((1 - mine) * reach, reach)),
+        (mine, pl.multiple_of(mine * reach, reach)),
+        (1 - mine, pl.multiple_of((1 - mine) * reach, reach)),
     )
     mask_bias = (mask[...].astype(F32) - 1.0) * 10000.0
     row_ones = by_head(jnp.ones((length, channels), BF16))
     lane_parts = channels // 128
-    for turn, (steps, which, start) in enumerate(turns):
-        gather_relay(0, bias_sem, bias_land, (), steps, 7 * turn)
-        gather_finish(7 * turn, bias_land, chips // 2)
+    for turn, (which, start) in enumerate(turns):
+        if turn == 0:
+            gather_forward(0, bias_sem.at[0], bias_land, 7)
+        taken(bias_land.at[pl.ds(0, half - 1)], recv_sem.at[7 * turn])
         fill(bias_f, landed(bias_land.at[pl.ds(which * half, half)]))
         extra = jnp.stack([pick(bias_f, h, reach, heads) for h in range(heads)], 0) + mask_bias
         gated = []
@@ -332,11 +315,7 @@
         part = (start // pack,)
         right_src[part[0]] = slab
         right_land[me, part[0]] = slab
-        forwarded = part[0] < rows // pack // 2
-        gather_start(
-            2, right_sem, right_src.at[part[0]], right_land, part,
-            chips // 2 if forwarded else None,
-        )
+        gather_start(2, right_sem.at[part[0]], right_src.at[part[0]], right_land, part)
 
     left = dot(jnp.concatenate(inputs, 0), factor_w[:width, :], NT).astype(BF16)
     chunk = 8
@@ -354,14 +333,10 @@
     fold = max(1, 128 // reach)
     height = pair_chan // fold
     normed = []
-    for turn, (steps, which, start) in enumerate(turns):
-        for k in range(rows // pack):
-            mirrored = k < rows // pack // 2
-            if turn == 0 and mirrored:
-                gather_forward(2, right_sem, right_land, (k,))
-            left_over = [x for x in steps if not (turn == 1 and mirrored and x == near)]
-            gather_relay(2, right_sem, right_land, (k,), left_over, 2 + 4 * turn)
-        gather_finish(2 + 4 * turn, right_land, chips // 2)
+    for k in range(rows // pack):
+        gather_forward(2, right_sem.at[k], right_land, 6, (k,))
+    for turn, (which, start) in enumerate(turns):
+        taken(right_land.at[pl.ds(0, half - 1)], recv_sem.at[2 + 4 * turn])
         fill(right_f, landed(right_land.at[pl.ds(which * half, half)]))
         for k in range(groups):
             right_m[:, k * lanes : (k + 1) * lanes] = pick(right_f, k, reach, groups).astype(BF16)
@@ -374,42 +349,43 @@
             pair_one_v[i, pl.ds(start, reach), :] = one
             stacked.append(one)
         normed.append(layer_normalized(jnp.concatenate(stacked, 0)).astype(BF16))
-        factors = dot(tri_t[...], normed[turn], NT)
-        for side, target in enumerate((tri_left, tri_right)):
+        for side, target in ((1, tri_right), (0, tri_left)):
             low = 2 * side * pair_chan
-            factor = (
-                jax.nn.sigmoid(factors[low + pair_chan : low + 2 * pair_chan])
-                * factors[low : low + pair_chan]
-            )
+            factors = dot(tri_t[low : low + 2 * pair_chan, :], normed[turn], NT)
+            factor = jax.nn.sigmoid(factors[pair_chan:]) * factors[:pair_chan]
             wide = fold * reach
             for base in range(rows // fold):
                 packed = pack_lanes(factor[:, base * wide : (base + 1) * wide], fold, reach)
                 for place in range(fold):
                     at = (base * fold + place) * height
-                    fill(tri_f.at[:, pl.ds(at, height), :], packed[place])
+                    fill(tri_f.at[side, :, pl.ds(at, height), :], packed[place])
             for g in range(half):
-                target[turn, g] = pick(tri_f, g, rows * own // fold, half).astype(BF16)
+                target[turn, g] = pick(
+                    tri_f.at[side], g, rows * own // fold, half
+                ).astype(BF16)
+            if side == 1:
+                spread(
+                    3,
+                    lambda peer: tri_right.at[turn, lax.rem(peer, half)],
+                    tri_land.at[which, me],
+                    everyone,
+                )
+            else:
+                spread(
+                    4,
+                    lambda peer: tri_left.at[turn, lax.rem(peer, half)],
+                    left_land.at[which, group],
+                    own_half,
+                )
         left_land[which, group] = tri_left[turn, group]
         tri_land[which, me] = tri_right[turn, group]
-        spread(
-            3,
-            lambda peer: tri_right.at[turn, lax.rem(peer, half)],
-            tri_land.at[which, me],
-            everyone,
-        )
-        spread(
-            4,
-            lambda peer: tri_left.at[turn, lax.rem(peer, half)],
-            left_land.at[which, group],
-            own_half,
-        )
 
     ordered = dot(to_output, jnp.concatenate(two_rows, 0))
     align_out[...] = ordered.reshape(total, rows, channels).astype(BF16)
     for turn in range(2):
         opened = jax.nn.sigmoid(dot(normed[turn], tri_w[:, 4 * pair_chan :]))
         for i in range(rows):
-            gate_v[i, pl.ds(turns[turn][2], reach), :] = opened[i * reach : (i + 1) * reach]
+            gate_v[i, pl.ds(turns[turn][1], reach), :] = opened[i * reach : (i + 1) * reach]
 
     taken(tri_land.at[pl.ds(0, 2), pl.ds(0, count - 1)], recv_sem.at[3])
     taken(left_land.at[pl.ds(0, 2), pl.ds(0, half - 1)], recv_sem.at[4])
@@ -465,15 +441,17 @@
     fill(back_f, landed(back_land))
     owners = back_land.shape[0]
     own = back_land.shape[1] // rows
+    stores = []
     for i in range(rows):
         channels = [pick(back_f, c * rows + i, owners, own * rows) for c in range(own)]
         combined = layer_normalized(jnp.concatenate(channels, 0), 0).astype(BF16)
         result = pair_one[i] + gate[i] * dot(combined, tri_o[...], TN)
         pair_v[i] = result.astype(BF16)
-    store_pair = pltpu.make_async_copy(pair_v, pair_out, sem.at[1])
-    store_pair.start()
+        stores.append(pltpu.make_async_copy(pair_v.at[i], pair_out.at[i], sem.at[1 + i]))
+        stores[i].start()
     store_align.wait()
-    store_pair.wait()
+    for store in stores:
+        store.wait()
 
 
 def shards(
@@ -552,7 +530,7 @@
             pieces(reach * groups, lanes),
             vmem((reach, width * total), BF16),
             vmem((4 * pair_chan, pair_chan), BF16),
-            pieces(rows * pair_chan // fold, fold * reach),
+            vmem((2, fold * reach // 128, rows * pair_chan // fold, 128), F32),
             pieces(2 * count * tri_slab[0], tri_slab[1]),
             pieces(2 * half * tri_slab[0], tri_slab[1]),
             pieces(half * own * rows, length),
@@ -563,8 +541,8 @@
             pltpu.SemaphoreType.DMA((len(operands),)),
             pltpu.SemaphoreType.DMA((6,)),
             pltpu.SemaphoreType.DMA((8,)),
-            pltpu.SemaphoreType.DMA((half - 1,)),
-            pltpu.SemaphoreType.DMA((parts, half - 1)),
+            pltpu.SemaphoreType.DMA((1,)),
+            pltpu.SemaphoreType.DMA((parts,)),
         ]
     )
     sizes = (count, seqs, rows, length, channels, heads, width, pair_chan, total)
@@ -596,7 +574,7 @@
         scratch_shapes=[
             pieces(half * own * rows, length),
             vmem(pair.shape, BF16),
-            pltpu.SemaphoreType.DMA((2,)),
+            pltpu.SemaphoreType.DMA((1 + rows,)),
         ],
         compiler_params=pltpu.CompilerParams(vmem_limit_bytes=VMEM_BYTES // 4),
     )(aligned, back, pair_one, gate, triangle_output_weight)

time: 42.8 us -> 41.9 us (0.979)
  Pallas kernels: 42 us -> 41.1 us
    pallas_call x1, Pallas kernels: 40.9 us -> 40 us  [shards(): pl.pallas_call(functools.partial(block_kernel, sizes), out_shape=(jax.Sha...]
where the time goes in v7:
time: 41.9 us; the launch traced here: 41.7 us
  Pallas kernels  41.1 us (98%)
  between operations  0.66 us (2%)
    pallas_call x1, Pallas kernels, shards(): pl.pallas_call(functools.partial(block_kernel, sizes), out_shape=(jax.Sha...  40 us
    pallas_call x1, Pallas kernels, shards(): pl.pallas_call(functools.partial(finish_kernel, rows), out_shape=(jax.Sha...  1.08 us

profile of v7, /device:TPU:0, one launch (start us, length us, event | category | flops | bytes accessed | tf_op | source)
XLA Modules:
  0.0 41.7 jit_solution(2574310103600441470)
XLA Ops:
  0.6 0.0 copy-start
  0.6 40.0 %shard_map.149 = (bf16[64,4,256]{2,1,0:T(4,128)(2,1)S(1)}, bf16[16,32,128]{2,1,0:T(8,128)(2,1)S(1)}, f32[4,128,128]{2,1,0:T(8,128)S(1)}, f32[4,128,128]{2,1,0:T(8,128)S(1)}) custom-call(s32[2,128]{1,0:T(2,128)} %ids_h.1, s32[1,128]{1,0:T(1,128)} %bitcast.5, bf16[2,128,256]{2,1,0:T(8,128)(2,1)} %align_h.1, bf16[4,128,128]{2,1,0:T(8,128)(2,1)} %pair_h.1, ...), custom_call_target="tpu_custom_call" | custom-call | tf_op jit(solution)/shard_map/pallas_call | solution.py:551
  40.7 0.0 copy-done
  40.7 1.1 %shard_map.150 = (bf16[64,4,256]{2,1,0:T(4,128)(2,1)}, bf16[4,128,128]{2,1,0:T(8,128)(2,1)}) custom-call(bf16[64,4,256]{2,1,0:T(4,128)(2,1)S(1)} %get-tuple-element.6.align, bf16[16,32,128]{2,1,0:T(8,128)(2,1)S(1)} %get-tuple-element.7.back_land, f32[4,128,128]{2,1,0:T(8,128)S(1)} %get-tuple-element.8.pair_one, f32[4,128,128]{2,1,0:T(8,128)S(1)} %get-tuple-element.9.gate, ...), custom_call_target="tpu_custom_call" | custom-call | tf_op jit(solution)/shard_map/pallas_call | solution.py:566
Async XLA Ops:
  0.6 40.0 %copy-start = (bf16[128,128]{1,0:T(8,128)(2,1)S(1)}, bf16[128,128]{1,0:T(8,128)(2,1)}, u32[]{:S(2)}) copy-start(bf16[128,128]{1,0:T(8,128)(2,1)} %tri_o.1) | copy-start | bytes 98308

commit v8 on v7

--- a/solution.py
+++ b/solution.py
@@ -114,7 +114,7 @@
     bias_src, bias_land, msa_src, msa_land, right_src, right_land, tri_left, left_land,
     tri_right, tri_land, back_src,
     bias_f, msa_f, outer_f, outer_w2, left_t, right_f, right_m, tri_t,
-    tri_f, land_f, left_f, comb_f, zero_v, raw_v, value_v, open_v,
+    tri_f, land_f, left_f, comb_f, zero_v, raw_v, value_v, open_v, column_v, project_v,
     in_sem, send_sem, recv_sem, bias_sem, right_sem,
 ):
     count, seqs, rows, length, channels, heads, width, pair_chan, total = sizes
@@ -171,10 +171,11 @@
 
     group = lax.rem(me, half)
 
-    def spread(number, source, landing, distances):
+    def spread(number, source, landing, distances, handed=None):
         for k in reversed(distances):
             peer = across(k)
-            remote(source(peer), landing, number, recv_sem.at[number], peer)
+            received_by = recv_sem.at[number if handed is None else handed]
+            remote(source(peer), landing, number, received_by, peer)
 
     everyone, own_half, other_half = range(1, count), range(1, half), range(half, count)
 
@@ -262,33 +263,42 @@
             lambda peer: msa_src.at[peer],
             msa_land.at[me],
             own_half if turn == 0 else other_half,
+            1 + 7 * turn,
         )
 
+    share = seqs * half
     to_output = selection(
         total * rows,
         lambda o: (
             split_index(o, rows)[1] * total
-            + split_index(split_index(o, rows)[0], seqs)[1] * count
-            + split_index(o, seqs * rows)[0]
+            + split_index(o, rows * share)[0] * share
+            + split_index(split_index(o, rows)[0], seqs)[1] * half
+            + split_index(split_index(o, rows * seqs)[0], half)[1]
         ),
     )
-    taken(msa_land.at[pl.ds(0, count - 1)], recv_sem.at[1])
-    fill(msa_f, landed(msa_land))
     step = lane_parts * seqs * rows
-    column = jnp.concatenate(
-        [
-            jnp.concatenate(
-                [
-                    pick(msa_f, (k * seqs + s) * rows + i, count, step)
-                    for i in range(rows)
-                    for s in range(seqs)
-                ],
-                0,
-            )
-            for k in range(lane_parts)
-        ],
-        1,
-    )
+    for turn, (which, start) in enumerate(turns):
+        taken(msa_land.at[pl.ds(0, half - 1 + turn)], recv_sem.at[1 + 7 * turn])
+        fill(msa_f, landed(msa_land.at[pl.ds(which * half, half)]))
+        column = jnp.concatenate(
+            [
+                jnp.concatenate(
+                    [
+                        pick(msa_f, (k * seqs + s) * rows + i, half, step)
+                        for i in range(rows)
+                        for s in range(seqs)
+                    ],
+                    0,
+                )
+                for k in range(lane_parts)
+            ],
+            1,
+        )
+        projected = dot(layer_normalized(column).astype(BF16), col_w[...])
+        place = pl.ds(pl.multiple_of(which * share, share), share)
+        for i in range(rows):
+            column_v[i, place, :] = column[i * share : (i + 1) * share]
+            project_v[i, place, :] = projected[i * share : (i + 1) * share]
     pack = max(1, 128 // total)
     groups = width // pack
     lanes = pack * total
@@ -299,9 +309,10 @@
     )
     two_rows, inputs = [], []
     for start in range(0, rows, pack):
-        block = column[start * total : (start + pack) * total]
-        projected = dot(layer_normalized(block).astype(BF16), col_w[...])
-        scores, value, opened = split(projected)
+        block = column_v[start : start + pack].reshape(lanes, channels)
+        scores, value, opened = split(
+            project_v[start : start + pack].reshape(lanes, 4 * channels)
+        )
         if pack > 1:
             scores = jnp.where(together, scores, -1e30)
         gated = (opened * attend(scores, value, column_ones)).astype(BF16)
@@ -523,7 +534,7 @@
         + exchanges
         + [
             pieces(half * heads * rows, length),
-            pieces(count * lane_parts * seqs * rows, 128),
+            pieces(half * lane_parts * seqs * rows, 128),
             pieces(width * width, pair_chan),
             vmem((width, width * pair_chan), BF16),
             vmem((width * total, rows * pair_chan), BF16),
@@ -538,9 +549,11 @@
             vmem((seqs, heads, length, length), F32),
             vmem((seqs, heads * length, channels), BF16),
             vmem((seqs, length, channels), F32),
+            vmem((rows, total, channels), F32),
+            vmem((rows, total, 4 * channels), F32),
             pltpu.SemaphoreType.DMA((len(operands),)),
             pltpu.SemaphoreType.DMA((6,)),
-            pltpu.SemaphoreType.DMA((8,)),
+            pltpu.SemaphoreType.DMA((9,)),
             pltpu.SemaphoreType.DMA((1,)),
             pltpu.SemaphoreType.DMA((parts,)),
         ]

time: 41.9 us -> 41.6 us (level)
  no operation moved by 1% of the time
where the time goes in v8:
time: 41.6 us; the launch traced here: 41.5 us
  Pallas kernels  40.8 us (98%)
  between operations  0.66 us (2%)
    pallas_call x1, Pallas kernels, shards(): pl.pallas_call(functools.partial(block_kernel, sizes), out_shape=(jax.Sha...  39.7 us
    pallas_call x1, Pallas kernels, shards(): pl.pallas_call(functools.partial(finish_kernel, rows), out_shape=(jax.Sha...  1.08 us

profile of v8, /device:TPU:0, one launch (start us, length us, event | category | flops | bytes accessed | tf_op | source)
XLA Modules:
  0.0 41.5 jit_solution(2128331720952444710)
XLA Ops:
  0.6 0.0 copy-start
  0.6 39.7 %shard_map.149 = (bf16[64,4,256]{2,1,0:T(4,128)(2,1)S(1)}, bf16[16,32,128]{2,1,0:T(8,128)(2,1)S(1)}, f32[4,128,128]{2,1,0:T(8,128)S(1)}, f32[4,128,128]{2,1,0:T(8,128)S(1)}) custom-call(s32[2,128]{1,0:T(2,128)} %ids_h.1, s32[1,128]{1,0:T(1,128)} %bitcast.5, bf16[2,128,256]{2,1,0:T(8,128)(2,1)} %align_h.1, bf16[4,128,128]{2,1,0:T(8,128)(2,1)} %pair_h.1, ...), custom_call_target="tpu_custom_call" | custom-call | tf_op jit(solution)/shard_map/pallas_call | solution.py:564
  40.4 0.0 copy-done
  40.4 1.1 %shard_map.150 = (bf16[64,4,256]{2,1,0:T(4,128)(2,1)}, bf16[4,128,128]{2,1,0:T(8,128)(2,1)}) custom-call(bf16[64,4,256]{2,1,0:T(4,128)(2,1)S(1)} %get-tuple-element.6.align, bf16[16,32,128]{2,1,0:T(8,128)(2,1)S(1)} %get-tuple-element.7.back_land, f32[4,128,128]{2,1,0:T(8,128)S(1)} %get-tuple-element.8.pair_one, f32[4,128,128]{2,1,0:T(8,128)S(1)} %get-tuple-element.9.gate, ...), custom_call_target="tpu_custom_call" | custom-call | tf_op jit(solution)/shard_map/pallas_call | solution.py:579
Async XLA Ops:
  0.6 39.8 %copy-start = (bf16[128,128]{1,0:T(8,128)(2,1)S(1)}, bf16[128,128]{1,0:T(8,128)(2,1)}, u32[]{:S(2)}) copy-start(bf16[128,128]{1,0:T(8,128)(2,1)} %tri_o.1) | copy-start | bytes 98308

commit v9 on v8

--- a/solution.py
+++ b/solution.py
@@ -189,6 +189,9 @@
     bias_src[...] = slab
     bias_land[me] = slab
 
+    pl.semaphore_wait(barrier, half)
+    gather_start(0, bias_sem.at[0], bias_src, bias_land)
+
     for load in loads[2:6]:
         load.wait()
     token = lax.broadcasted_iota(jnp.int32, (table.shape[0], length), 0)
@@ -216,9 +219,6 @@
     zero_v[...] = msa_zero.reshape(zero_v.shape)
     for s in range(seqs):
         raw_v[s], value_v[s], open_v[s] = split(projected[s * length : (s + 1) * length])
-    pl.semaphore_wait(barrier, half)
-    gather_start(0, bias_sem.at[0], bias_src, bias_land)
-
     for load in loads[8:]:
         load.wait()
     tri_t[...] = jnp.transpose(tri_w[:, : 4 * pair_chan].astype(F32), (1, 0)).astype(BF16)

time: 41.6 us -> 41.4 us (level)
  no operation moved by 1% of the time
where the time goes in v9:
time: 41.4 us; the launch traced here: 41.2 us
  Pallas kernels  40.5 us (98%)
  between operations  0.66 us (2%)
    pallas_call x1, Pallas kernels, shards(): pl.pallas_call(functools.partial(block_kernel, sizes), out_shape=(jax.Sha...  39.5 us
    pallas_call x1, Pallas kernels, shards(): pl.pallas_call(functools.partial(finish_kernel, rows), out_shape=(jax.Sha...  1.08 us

profile of v9, /device:TPU:0, one launch (start us, length us, event | category | flops | bytes accessed | tf_op | source)
XLA Modules:
  0.0 41.2 jit_solution(15611853937625729880)
XLA Ops:
  0.6 0.0 copy-start
  0.6 39.5 %shard_map.149 = (bf16[64,4,256]{2,1,0:T(4,128)(2,1)S(1)}, bf16[16,32,128]{2,1,0:T(8,128)(2,1)S(1)}, f32[4,128,128]{2,1,0:T(8,128)S(1)}, f32[4,128,128]{2,1,0:T(8,128)S(1)}) custom-call(s32[2,128]{1,0:T(2,128)} %ids_h.1, s32[1,128]{1,0:T(1,128)} %bitcast.5, bf16[2,128,256]{2,1,0:T(8,128)(2,1)} %align_h.1, bf16[4,128,128]{2,1,0:T(8,128)(2,1)} %pair_h.1, ...), custom_call_target="tpu_custom_call" | custom-call | tf_op jit(solution)/shard_map/pallas_call | solution.py:564
  40.1 0.0 copy-done
  40.1 1.1 %shard_map.150 = (bf16[64,4,256]{2,1,0:T(4,128)(2,1)}, bf16[4,128,128]{2,1,0:T(8,128)(2,1)}) custom-call(bf16[64,4,256]{2,1,0:T(4,128)(2,1)S(1)} %get-tuple-element.6.align, bf16[16,32,128]{2,1,0:T(8,128)(2,1)S(1)} %get-tuple-element.7.back_land, f32[4,128,128]{2,1,0:T(8,128)S(1)} %get-tuple-element.8.pair_one, f32[4,128,128]{2,1,0:T(8,128)S(1)} %get-tuple-element.9.gate, ...), custom_call_target="tpu_custom_call" | custom-call | tf_op jit(solution)/shard_map/pallas_call | solution.py:579
Async XLA Ops:
  0.6 39.5 %copy-start = (bf16[128,128]{1,0:T(8,128)(2,1)S(1)}, bf16[128,128]{1,0:T(8,128)(2,1)}, u32[]{:S(2)}) copy-start(bf16[128,128]{1,0:T(8,128)(2,1)} %tri_o.1) | copy-start | bytes 98308

commit v10 on v9

--- a/solution.py
+++ b/solution.py
@@ -82,9 +82,12 @@
 
 
 def attend(scores, values, ones):
-    powers = jnp.exp(scores - jnp.max(scores, -1, keepdims=True)).astype(BF16)
-    side = jnp.concatenate([powers[h] for h in range(powers.shape[0])], 1)
-    return dot(side, values) / dot(side, ones)
+    sides = []
+    for block in scores:
+        powers = jnp.exp(block - jnp.max(block, -1, keepdims=True)).astype(BF16)
+        sides.append(jnp.concatenate([powers[h] for h in range(powers.shape[0])], 1))
+    mixed = jnp.concatenate([dot(side, value) for side, value in zip(sides, values)], 0)
+    return mixed / dot(jnp.concatenate(sides, 0), ones)
 
 
 def interleave(blocks, rows):
@@ -243,11 +246,13 @@
         taken(bias_land.at[pl.ds(0, half - 1)], recv_sem.at[7 * turn])
         fill(bias_f, landed(bias_land.at[pl.ds(which * half, half)]))
         extra = jnp.stack([pick(bias_f, h, reach, heads) for h in range(heads)], 0) + mask_bias
-        gated = []
-        for s in range(seqs):
-            mixed = attend(raw_v[s, :, pl.ds(start, reach), :] + extra, value_v[s], row_ones)
-            gated.append((open_v[s, pl.ds(start, reach), :] * mixed).astype(BF16))
-        added = dot(jnp.concatenate(gated, 0), row_o[...])
+        mixed = attend(
+            [raw_v[s, :, pl.ds(start, reach), :] + extra for s in range(seqs)],
+            [value_v[s] for s in range(seqs)],
+            row_ones,
+        )
+        opened = open_v[:, pl.ds(start, reach), :].reshape(mixed.shape)
+        added = dot((opened * mixed).astype(BF16), row_o[...])
         blocks = [
             zero_v[s, pl.ds(start, reach), :] + added[s * reach : (s + 1) * reach]
             for s in range(seqs)
@@ -315,7 +320,7 @@
         )
         if pack > 1:
             scores = jnp.where(together, scores, -1e30)
-        gated = (opened * attend(scores, value, column_ones)).astype(BF16)
+        gated = (opened * attend([scores], [value], column_ones)).astype(BF16)
         msa_two = block + dot(gated, col_o[...])
         outer_input = layer_normalized(msa_two).astype(BF16)
         two_rows.append(msa_two.astype(BF16))
@@ -452,17 +457,21 @@
     fill(back_f, landed(back_land))
     owners = back_land.shape[0]
     own = back_land.shape[1] // rows
-    stores = []
-    for i in range(rows):
-        channels = [pick(back_f, c * rows + i, owners, own * rows) for c in range(own)]
-        combined = layer_normalized(jnp.concatenate(channels, 0), 0).astype(BF16)
-        result = pair_one[i] + gate[i] * dot(combined, tri_o[...], TN)
-        pair_v[i] = result.astype(BF16)
-        stores.append(pltpu.make_async_copy(pair_v.at[i], pair_out.at[i], sem.at[1 + i]))
-        stores[i].start()
+    combined = jnp.concatenate(
+        [
+            jnp.concatenate(
+                [pick(back_f, c * rows + i, owners, own * rows) for c in range(own)], 0
+            )
+            for i in range(rows)
+        ],
+        1,
+    )
+    added = dot(layer_normalized(combined, 0).astype(BF16), tri_o[...], TN)
+    pair_v[...] = (pair_one[...] + gate[...] * added.reshape(gate.shape)).astype(BF16)
+    store_pair = pltpu.make_async_copy(pair_v, pair_out, sem.at[1])
+    store_pair.start()
     store_align.wait()
-    for store in stores:
-        store.wait()
+    store_pair.wait()
 
 
 def shards(
@@ -587,7 +596,7 @@
         scratch_shapes=[
             pieces(half * own * rows, length),
             vmem(pair.shape, BF16),
-            pltpu.SemaphoreType.DMA((1 + rows,)),
+            pltpu.SemaphoreType.DMA((2,)),
         ],
         compiler_params=pltpu.CompilerParams(vmem_limit_bytes=VMEM_BYTES // 4),
     )(aligned, back, pair_one, gate, triangle_output_weight)

time: 41.4 us -> 41.4 us (level)
  no operation moved by 1% of the time
where the time goes in v10:
time: 41.4 us; the launch traced here: 41.2 us
  Pallas kernels  40.5 us (98%)
  between operations  0.66 us (2%)
    pallas_call x1, Pallas kernels, shards(): pl.pallas_call(functools.partial(block_kernel, sizes), out_shape=(jax.Sha...  39.5 us
    pallas_call x1, Pallas kernels, shards(): pl.pallas_call(functools.partial(finish_kernel, rows), out_shape=(jax.Sha...  1.08 us

profile of v10, /device:TPU:0, one launch (start us, length us, event | category | flops | bytes accessed | tf_op | source)
XLA Modules:
  0.0 41.2 jit_solution(3605500661680025291)
XLA Ops:
  0.6 0.0 copy-start
  0.6 39.5 %shard_map.149 = (bf16[64,4,256]{2,1,0:T(4,128)(2,1)S(1)}, bf16[16,32,128]{2,1,0:T(8,128)(2,1)S(1)}, f32[4,128,128]{2,1,0:T(8,128)S(1)}, f32[4,128,128]{2,1,0:T(8,128)S(1)}) custom-call(s32[2,128]{1,0:T(2,128)} %ids_h.1, s32[1,128]{1,0:T(1,128)} %bitcast.5, bf16[2,128,256]{2,1,0:T(8,128)(2,1)} %align_h.1, bf16[4,128,128]{2,1,0:T(8,128)(2,1)} %pair_h.1, ...), custom_call_target="tpu_custom_call" | custom-call | tf_op jit(solution)/shard_map/pallas_call | solution.py:573
  40.1 0.0 copy-done
  40.1 1.1 %shard_map.150 = (bf16[64,4,256]{2,1,0:T(4,128)(2,1)}, bf16[4,128,128]{2,1,0:T(8,128)(2,1)}) custom-call(bf16[64,4,256]{2,1,0:T(4,128)(2,1)S(1)} %get-tuple-element.6.align, bf16[16,32,128]{2,1,0:T(8,128)(2,1)S(1)} %get-tuple-element.7.back_land, f32[4,128,128]{2,1,0:T(8,128)S(1)} %get-tuple-element.8.pair_one, f32[4,128,128]{2,1,0:T(8,128)S(1)} %get-tuple-element.9.gate, ...), custom_call_target="tpu_custom_call" | custom-call | tf_op jit(solution)/shard_map/pallas_call | solution.py:588
Async XLA Ops:
  0.6 39.5 %copy-start = (bf16[128,128]{1,0:T(8,128)(2,1)S(1)}, bf16[128,128]{1,0:T(8,128)(2,1)}, u32[]{:S(2)}) copy-start(bf16[128,128]{1,0:T(8,128)(2,1)} %tri_o.1) | copy-start | bytes 98308
